TPU v7x, 32 devices: a whole 2x2x4 slice. The times are simulated.
32 devices in a mesh: dp: 8 (over z, x), mp: 4 (over y, core).
Axes of the slice: x: 2, y: 2, z: 4, core: 2. Of those that a mesh axis runs over, the one named last changes fastest.
Arguments:
- hidden_in: bfloat16 [8192, 1024], P(('dp', 'mp')), may hold values from -6 to 6
- doc_index: int32 [8192], P('dp'), may hold values from 0 to 256, as said below
- doc_position: int32 [8192], P('dp'), may hold values from 0 to 767, as said below
- w_query: bfloat16 [1024, 1024], P(None, 'mp'), may hold values from -0.1875 to 0.1875
- w_key: bfloat16 [1024, 1024], P(None, 'mp'), may hold values from -0.1875 to 0.1875
- w_value: bfloat16 [1024, 1024], P(None, 'mp'), may hold values from -0.1875 to 0.1875
- w_out: bfloat16 [1024, 1024], P('mp'), may hold values from -0.1875 to 0.1875
- w_up: bfloat16 [1024, 4096], P(None, 'mp'), may hold values from -0.1875 to 0.1875
- w_gate: bfloat16 [1024, 4096], P(None, 'mp'), may hold values from -0.1875 to 0.1875
- w_down: bfloat16 [4096, 1024], P('mp'), may hold values from -0.09375 to 0.09375
- score_scale: float32 [1024], P('mp'), may hold values from 1 to 1.7
- up_scale: float32 [4096], P('mp'), may hold values from 0.5 to 2
- gate_scale: float32 [4096], P('mp'), may hold values from 0.5 to 2
- alpha_attention: float32 [1024], replicated, may hold values from 0.2 to 0.6
- alpha_feedforward: float32 [1024], replicated, may hold values from 0.2 to 0.6
- cotangent: bfloat16 [8192, 1024], P(('dp', 'mp'))
Outputs:
- layer_out: bfloat16 [8192, 1024], P(('dp', 'mp'))
- grad_input: float32 [8192, 1024], P(('dp', 'mp'))
- grad_query: float32 [1024, 1024], P('dp', 'mp')
- grad_key: float32 [1024, 1024], P('dp', 'mp')
- grad_value: float32 [1024, 1024], P('dp', 'mp')
- grad_out: float32 [1024, 1024], P('mp', 'dp')
- grad_up: float32 [1024, 4096], P('dp', 'mp')
- grad_gate: float32 [1024, 4096], P('dp', 'mp')
- grad_down: float32 [4096, 1024], P('mp', 'dp')
- grad_score_scale: float32 [1024], P(('mp', 'dp'))
- grad_up_scale: float32 [4096], P(('mp', 'dp'))
- grad_gate_scale: float32 [4096], P(('mp', 'dp'))
- grad_alpha_attention: float32 [1024], P(('mp', 'dp'))
- grad_alpha_feedforward: float32 [1024], P(('mp', 'dp'))
Inputs may be any that keep to these rules, and one draw needn't show every extreme that they name: `doc_index`: within each sequence of 1024 tokens, document numbers start at 0 on its first token and rise by one at each document start; one document of exactly 768 tokens begins within the sequence's first 256 tokens and ends within its last 256. `doc_position`: counts tokens from 0 at the first token of each document.
All inputs are finite; a program needn't handle non-finite values.
Results may differ from a plain program's by a relative error of at most 0.025.
Values may be sent and summed in bfloat16 or wider, within the bound.
No kernel may reach another device: no remote copies, remote signals or barrier semaphores. Data moves between devices by JAX's collectives and lax.ppermute only.
A program may use at most 128 MiB of HBM per device.

v0:
```python
from functools import partial

import jax
import jax.numpy as jnp
from jax import lax
from jax.sharding import PartitionSpec as P

HEAD_DIM = 64


epsilon = 1e-06
masked_fill = -1e30


def sphere(values):
    return values * lax.rsqrt(jnp.mean(values * values, axis=-1, keepdims=True) + epsilon)


def rotate(values, positions):
    half_dim = values.shape[-1] // 2
    steps_half = jnp.arange(half_dim).astype(jnp.float32)
    inverse = jnp.exp(steps_half * (-2.0 * jnp.log(10000.0) / values.shape[-1]))
    angles = positions.astype(jnp.float32)[:, None] * inverse[None, :]
    cosine = jnp.cos(angles)[:, None, :]
    sine = jnp.sin(angles)[:, None, :]
    first_half = values[..., :half_dim]
    second_half = values[..., half_dim:]
    return jnp.concatenate(
        [first_half * cosine - second_half * sine, second_half * cosine + first_half * sine],
        axis=-1,
    )


def prepare(positions, query0, key0, score_scale):
    seq_len = query0.shape[0]
    local_heads = score_scale.shape[0] // HEAD_DIM
    head_shape = (seq_len, local_heads, HEAD_DIM)
    scales = score_scale.reshape(local_heads, HEAD_DIM)
    return (
        sphere(rotate(query0.reshape(head_shape), positions)) * scales,
        sphere(rotate(key0.reshape(head_shape), positions)) * scales,
    )


def sphere_update(residual, mixed, alpha):
    return sphere(residual + alpha * (sphere(mixed) - residual))


def gated_unit(up_proj, gate_proj, up_scale, gate_scale):
    return up_proj * up_scale * jax.nn.silu(gate_proj * gate_scale)


def masked_scores(query_block, key_heads, doc_rows, first_row):
    block_rows = query_block.shape[1]
    seq_len = key_heads.shape[1]
    scale_factor = 1.0 / query_block.shape[2] ** 0.5
    row_index = first_row + jnp.arange(block_rows)
    col_index = jnp.arange(seq_len)
    row_docs = lax.dynamic_slice_in_dim(doc_rows, first_row, block_rows, 0)
    allowed = (row_docs[:, None] == doc_rows[None, :]) & (col_index[None, :] <= row_index[:, None])
    raw_scores = jnp.einsum(
        "hqd,hkd->hqk", query_block, key_heads, preferred_element_type=jnp.float32
    )
    return (jnp.where(allowed[None], raw_scores * scale_factor, masked_fill), scale_factor)


def attend_forward(queries, key_heads, value_heads, doc_rows):
    local_heads, seq_len, head_dim = queries.shape
    block_rows = 512

    def one_block(first_row):
        query_block = lax.dynamic_slice_in_dim(queries, first_row, block_rows, 1)
        scores, scale_factor = masked_scores(query_block, key_heads, doc_rows, first_row)
        row_max = jnp.max(scores, axis=-1, keepdims=True)
        exponent = jnp.exp(scores - row_max)
        row_sum = jnp.sum(exponent, axis=-1, keepdims=True)
        probability = (exponent / row_sum).astype(jnp.bfloat16)
        attended = jnp.einsum(
            "hqk,hkd->hqd", probability, value_heads, preferred_element_type=jnp.float32
        )
        return (attended, row_max + jnp.log(row_sum))

    firsts = jnp.arange(seq_len // block_rows) * block_rows
    attended, log_total = lax.map(one_block, firsts)
    attended = jnp.transpose(attended, (0, 2, 1, 3)).reshape(seq_len, local_heads * head_dim)
    return (attended, log_total)


def attend_backward(queries, key_heads, value_heads, doc_rows, log_total, grad_heads):
    seq_len = queries.shape[1]
    block_rows = 512

    def one_block(carry, inputs):
        grad_keys, grad_values = carry
        first_row, block_total = inputs
        query_block = lax.dynamic_slice_in_dim(queries, first_row, block_rows, 1)
        grad_block = lax.dynamic_slice_in_dim(grad_heads, first_row, block_rows, 1)
        scores, scale_factor = masked_scores(query_block, key_heads, doc_rows, first_row)
        probability = jnp.exp(scores - block_total)
        grad_prob = jnp.einsum(
            "hqd,hkd->hqk", grad_block, value_heads, preferred_element_type=jnp.float32
        )
        inner_sum = jnp.sum(probability * grad_prob, axis=-1, keepdims=True)
        grad_scores = (probability * (grad_prob - inner_sum) * scale_factor).astype(jnp.bfloat16)
        grad_query = jnp.einsum(
            "hqk,hkd->hqd", grad_scores, key_heads, preferred_element_type=jnp.float32
        )
        grad_keys = grad_keys + jnp.einsum(
            "hqk,hqd->hkd", grad_scores, query_block, preferred_element_type=jnp.float32
        )
        grad_values = grad_values + jnp.einsum(
            "hqk,hqd->hkd",
            probability.astype(jnp.bfloat16),
            grad_block,
            preferred_element_type=jnp.float32,
        )
        return ((grad_keys, grad_values), grad_query)

    firsts = jnp.arange(seq_len // block_rows) * block_rows
    zeros_heads = jnp.zeros(key_heads.shape, jnp.float32)
    (grad_keys, grad_values), grad_query = lax.scan(
        one_block, (zeros_heads, zeros_heads), (firsts, log_total)
    )
    grad_query = jnp.transpose(grad_query, (1, 0, 2, 3)).reshape(queries.shape)
    return (grad_query, grad_keys, grad_values)


def body(
    hidden_in,
    doc_index,
    doc_position,
    w_query,
    w_key,
    w_value,
    w_out,
    w_up,
    w_gate,
    w_down,
    score_scale,
    up_scale,
    gate_scale,
    alpha_attention,
    alpha_feedforward,
    cotangent,
):
    head_width = w_query.shape[1]
    local_heads = head_width // HEAD_DIM
    ff_width = w_up.shape[1]
    residual = hidden_in.astype(jnp.float32)
    seq_rows = lax.all_gather(hidden_in, "mp", axis=0, tiled=True)
    seq_len = seq_rows.shape[0]
    w_joint = jnp.concatenate([w_query, w_key, w_value], axis=1)
    joint_proj = jnp.dot(seq_rows, w_joint, preferred_element_type=jnp.float32)
    query0 = joint_proj[:, :head_width]
    key0 = joint_proj[:, head_width : 2 * head_width]
    value0 = joint_proj[:, 2 * head_width :]
    (query_norm, key_norm), prepare_pull = jax.vjp(
        partial(prepare, doc_position), query0, key0, score_scale
    )
    queries = query_norm.astype(jnp.bfloat16).transpose(1, 0, 2)
    key_heads = key_norm.astype(jnp.bfloat16).transpose(1, 0, 2)
    value_heads = (
        value0.astype(jnp.bfloat16).reshape(seq_len, local_heads, HEAD_DIM).transpose(1, 0, 2)
    )
    attended, log_total = attend_forward(queries, key_heads, value_heads, doc_index)
    attended_low = attended.astype(jnp.bfloat16)
    mixed_attn = lax.psum_scatter(
        jnp.dot(attended_low, w_out, preferred_element_type=jnp.float32).astype(jnp.bfloat16),
        "mp",
        scatter_dimension=0,
        tiled=True,
    ).astype(jnp.float32)
    middle, middle_pull = jax.vjp(sphere_update, residual, mixed_attn, alpha_attention)
    middle_low = middle.astype(jnp.bfloat16)
    mid_rows = lax.all_gather(middle_low, "mp", axis=0, tiled=True)
    w_pair = jnp.concatenate([w_up, w_gate], axis=1)
    pair_proj = jnp.dot(mid_rows, w_pair, preferred_element_type=jnp.float32)
    inner, inner_pull = jax.vjp(
        gated_unit, pair_proj[:, :ff_width], pair_proj[:, ff_width:], up_scale, gate_scale
    )
    inner_low = inner.astype(jnp.bfloat16)
    mixed_ff = lax.psum_scatter(
        jnp.dot(inner_low, w_down, preferred_element_type=jnp.float32).astype(jnp.bfloat16),
        "mp",
        scatter_dimension=0,
        tiled=True,
    ).astype(jnp.float32)
    layer_out, out_pull = jax.vjp(sphere_update, middle, mixed_ff, alpha_feedforward)
    grad_middle_res, grad_mixed_ff, grad_alpha_ff = out_pull(cotangent.astype(jnp.float32))
    grad_mix_rows = lax.all_gather(grad_mixed_ff.astype(jnp.bfloat16), "mp", axis=0, tiled=True)
    grad_inner = jnp.einsum("sd,fd->sf", grad_mix_rows, w_down, preferred_element_type=jnp.float32)
    grad_w_down = jnp.einsum(
        "sf,sd->fd", inner_low, grad_mix_rows, preferred_element_type=jnp.float32
    )
    grad_up0, grad_gate0, grad_up_scale, grad_gate_scale = inner_pull(grad_inner)
    grad_pair = jnp.concatenate([grad_up0, grad_gate0], axis=1).astype(jnp.bfloat16)
    grad_middle_mm = lax.psum_scatter(
        jnp.einsum("sc,dc->sd", grad_pair, w_pair, preferred_element_type=jnp.float32).astype(
            jnp.bfloat16
        ),
        "mp",
        scatter_dimension=0,
        tiled=True,
    ).astype(jnp.float32)
    grad_w_pair = jnp.einsum("sd,sc->dc", mid_rows, grad_pair, preferred_element_type=jnp.float32)
    grad_resid_attn, grad_mixed_attn, grad_alpha_attn = middle_pull(
        grad_middle_res + grad_middle_mm
    )
    grad_mixed_low = grad_mixed_attn.astype(jnp.bfloat16)
    grad_rows_all = lax.all_gather(grad_mixed_low, "mp", axis=0, tiled=True)
    grad_attended = jnp.einsum(
        "sd,hd->sh", grad_rows_all, w_out, preferred_element_type=jnp.float32
    ).astype(jnp.bfloat16)
    grad_w_out = jnp.einsum(
        "sh,sd->hd", attended_low, grad_rows_all, preferred_element_type=jnp.float32
    )
    grad_heads = grad_attended.reshape(seq_len, local_heads, HEAD_DIM).transpose(1, 0, 2)
    grad_q_heads, grad_k_heads, grad_v_heads = attend_backward(
        queries, key_heads, value_heads, doc_index, log_total, grad_heads
    )
    grad_query0, grad_key0, grad_score_scale = prepare_pull(
        (grad_q_heads.transpose(1, 0, 2), grad_k_heads.transpose(1, 0, 2))
    )
    grad_value0 = grad_v_heads.transpose(1, 0, 2).reshape(seq_len, head_width)
    grad_joint = jnp.concatenate([grad_query0, grad_key0, grad_value0], axis=1).astype(jnp.bfloat16)
    grad_seq = jnp.einsum("sc,dc->sd", grad_joint, w_joint, preferred_element_type=jnp.float32)
    grad_w_joint = jnp.einsum("sd,sc->dc", seq_rows, grad_joint, preferred_element_type=jnp.float32)
    grad_alphas = jnp.stack([grad_alpha_attn, grad_alpha_ff])
    grad_own, alpha_share = (
        lax.psum_scatter(
            grad_seq.astype(jnp.bfloat16), "mp", scatter_dimension=0, tiled=True
        ).astype(jnp.float32),
        lax.psum_scatter(
            grad_alphas.astype(jnp.bfloat16), "mp", scatter_dimension=1, tiled=True
        ).astype(jnp.float32),
    )
    grad_input = grad_resid_attn + grad_own
    (
        joint_share,
        out_share,
        pair_share,
        down_share,
        score_share,
        up_share,
        gate_share,
        alpha_final,
    ) = (
        lax.psum_scatter(
            grad_w_joint.astype(jnp.bfloat16), "dp", scatter_dimension=0, tiled=True
        ).astype(jnp.float32),
        lax.psum_scatter(
            grad_w_out.astype(jnp.bfloat16), "dp", scatter_dimension=1, tiled=True
        ).astype(jnp.float32),
        lax.psum_scatter(
            grad_w_pair.astype(jnp.bfloat16), "dp", scatter_dimension=0, tiled=True
        ).astype(jnp.float32),
        lax.psum_scatter(
            grad_w_down.astype(jnp.bfloat16), "dp", scatter_dimension=1, tiled=True
        ).astype(jnp.float32),
        lax.psum_scatter(
            grad_score_scale.astype(jnp.bfloat16), "dp", scatter_dimension=0, tiled=True
        ).astype(jnp.float32),
        lax.psum_scatter(
            grad_up_scale.astype(jnp.bfloat16), "dp", scatter_dimension=0, tiled=True
        ).astype(jnp.float32),
        lax.psum_scatter(
            grad_gate_scale.astype(jnp.bfloat16), "dp", scatter_dimension=0, tiled=True
        ).astype(jnp.float32),
        lax.psum_scatter(
            alpha_share.astype(jnp.bfloat16), "dp", scatter_dimension=1, tiled=True
        ).astype(jnp.float32),
    )
    return (
        layer_out.astype(jnp.bfloat16),
        grad_input,
        joint_share[:, :head_width],
        joint_share[:, head_width : 2 * head_width],
        joint_share[:, 2 * head_width :],
        out_share,
        pair_share[:, :ff_width],
        pair_share[:, ff_width:],
        down_share,
        score_share,
        up_share,
        gate_share,
        alpha_final[0],
        alpha_final[1],
    )


def solution(mesh):
    return jax.shard_map(
        body,
        mesh=mesh,
        in_specs=(
            P(("dp", "mp"), None),
            P("dp"),
            P("dp"),
            P(None, "mp"),
            P(None, "mp"),
            P(None, "mp"),
            P("mp", None),
            P(None, "mp"),
            P(None, "mp"),
            P("mp", None),
            P("mp"),
            P("mp"),
            P("mp"),
            P(),
            P(),
            P(("dp", "mp"), None),
        ),
        out_specs=(
            P(("dp", "mp"), None),
            P(("dp", "mp"), None),
            P("dp", "mp"),
            P("dp", "mp"),
            P("dp", "mp"),
            P("mp", "dp"),
            P("dp", "mp"),
            P("dp", "mp"),
            P("mp", "dp"),
            P(("mp", "dp")),
            P(("mp", "dp")),
            P(("mp", "dp")),
            P(("mp", "dp")),
            P(("mp", "dp")),
        ),
        check_vma=False,
    )
```

profile of v0, /device:TPU:0, one launch (start us, length us, event | category | flops | bytes accessed | tf_op | source)
XLA Modules:
  0.0 712.1 jit_solution(7154638728471889156)
XLA Ops:
  10.3 2.0 constant_dynamic-update-slice_fusion.2
  12.2 2.0 constant_dynamic-update-slice_fusion.1
  14.2 1.9 constant_dynamic-update-slice_fusion
  16.7 18.2 %all-gather.5.cloned.1.call-done = bf16[1024,1024]{1,0:T(8,128)(2,1)} async-done(((bf16[256,1024]{1,0:T(8,128)(2,1)}), bf16[1024,1024]{1,0:T(8,128)(2,1)}) %all-gather.5.cloned.1.call-update) | async-done | bytes 2097168 | tf_op jit(solution)/shard_map/all_gather | solution.py:150
  34.9 3.9 convolution_bitcast_fusion
  41.8 26.0 %while.29 = (s32[]{:T(128)}, bf16[2,4,512,64]{2,3,1,0:T(8,128)(2,1)}, f32[2,4,512,1]{2,1,3,0:T(4,128)S(1)}, s32[2]{0:T(128)S(1)}, s32[1024]{0:T(1024)S(1)}, /*in...) while((s32[]{:T(128)}, ...), condition=%wide.region_5.6_spmd.clone, body=%wide.region_2.5_spmd.sunk.clone | while | flops 563608064 | bytes 33372376 | solution.py:84
  45.7 3.0 fusion.181
  48.7 2.3 fusion.182
  51.0 3.0 fusion.183
  58.7 3.0 fusion.181
  61.7 2.3 fusion.182
  64.0 3.0 fusion.183
  67.9 1.8 copy.38
  70.5 3.1 convolution_convert_fusion.3
  73.7 31.5 %reduce-scatter.21.cloned.1.call-done = bf16[256,1024]{1,0:T(8,128)(2,1)} async-done(((bf16[1024,1024]{1,0:T(8,128)(2,1)}), bf16[256,1024]{1,0:T(8,128)(2,1)}) %reduce-scatter.21.cloned.1.call-update) | async-done | bytes 524304 | tf_op jit(solution)/shard_map/reduce_scatter | solution.py:167
  106.5 1.7 multiply_reduce_fusion.9
  108.2 2.4 multiply_convert_fusion.7
  111.1 3.3 constant_dynamic-update-slice_fusion.4
  114.5 1.6 constant_dynamic-update-slice_fusion.3
  116.0 17.4 %all-gather.7.cloned.1.call-done = bf16[1024,1024]{1,0:T(8,128)(2,1)} async-done(((bf16[256,1024]{1,0:T(8,128)(2,1)}), bf16[1024,1024]{1,0:T(8,128)(2,1)}) %all-gather.7.cloned.1.call-update) | async-done | bytes 2097168 | tf_op jit(solution)/shard_map/all_gather | solution.py:175
  133.4 6.9 fusion.108
  141.7 2.1 copy-done.21
  145.0 3.7 convolution_convert_fusion.2
  148.8 31.5 %reduce-scatter.23.cloned.1.call-done = bf16[256,1024]{1,0:T(8,128)(2,1)} async-done(((bf16[1024,1024]{1,0:T(8,128)(2,1)}), bf16[256,1024]{1,0:T(8,128)(2,1)}) %reduce-scatter.23.cloned.1.call-update) | async-done | bytes 524304 | tf_op jit(solution)/shard_map/reduce_scatter | solution.py:182
  181.6 2.2 fusion.82
  183.9 2.4 fusion.89
  188.4 22.7 %all-gather.9.cloned.1.call-done = bf16[1024,1024]{1,0:T(8,128)(2,1)} async-done(((bf16[256,1024]{1,0:T(8,128)(2,1)}), bf16[1024,1024]{1,0:T(8,128)(2,1)}) %all-gather.9.cloned.1.call-update) | async-done | bytes 2097168 | tf_op jit(solution)/shard_map/all_gather | solution.py:190
  211.1 7.8 %multiply_reduce_fusion.1 = (bf16[1024]{0:T(1024)(128)(2,1)S(1)}, bf16[1024]{0:T(1024)(128)(2,1)S(1)}, f32[1024,1024]{1,0:T(8,128)S(1)}, bf16[1024,1024]{1,0:T(8,128)(2,1)S(1)}) fusion(f32[1024,2048]{1,0:T(8,128)} %copy-done.21, f32[1024]{0:T(1024)S(1)} %copy-done.54, f32[1024]{0:T(1024)S(1)} %copy-done.55, ...), kind=kOutput, calls=%fused_computation.65 | convolution fusion | flops 2168453120 | bytes 18886656 | tf_op jit(solution)/shard_map/sd,fd->sf/dot_general | solution.py:191
  220.9 8.1 %fusion.80 = bf16[1024,1024]{1,0:T(8,128)(2,1)} fusion(bf16[1024,2048]{1,0:T(8,128)(2,1)} %constant_dynamic-update-slice_fusion.3, bf16[1024,1024]{1,0:T(8,128)(2,1)S(1)} %multiply_convert_fusion.1, bf16[1024,1024]{1,0:T(8,128)(2,1)S(1)} %get-tuple-element.259), kind=kOutput, calls=%fused_computation.76 | convolution fusion | flops 4304404480 | bytes 10485760 | tf_op jit(solution)/shard_map/sc,dc->sd/dot_general | solution.py:198
  229.2 31.4 %reduce-scatter.25.cloned.1.call-done = bf16[256,1024]{1,0:T(8,128)(2,1)} async-done(((bf16[1024,1024]{1,0:T(8,128)(2,1)}), bf16[256,1024]{1,0:T(8,128)(2,1)}) %reduce-scatter.25.cloned.1.call-update) | async-done | bytes 524304 | tf_op jit(solution)/shard_map/reduce_scatter | solution.py:197
  260.6 1.9 multiply_reduce_fusion.3
  262.5 2.9 multiply_reduce_fusion.4
  266.4 2.3 fusion.84
  268.8 4.6 convolution_convert_fusion.1
  273.4 2.6 copy.47
  276.1 10.5 %reduce-scatter.37.cloned.1.call-done = bf16[256,2]{1,0:T(8,128)(2,1)} async-done(((bf16[1024,2]{1,0:T(8,128)(2,1)}), bf16[256,2]{1,0:T(8,128)(2,1)}) %reduce-scatter.37.cloned.1.call-update) | async-done | bytes 1040
  286.7 24.7 %all-gather.11.cloned.1.call-done = bf16[1024,1024]{1,0:T(8,128)(2,1)} async-done(((bf16[256,1024]{1,0:T(8,128)(2,1)}), bf16[1024,1024]{1,0:T(8,128)(2,1)}) %all-gather.11.cloned.1.call-update) | async-done | bytes 2097168 | tf_op jit(solution)/shard_map/all_gather | solution.py:210
  311.3 3.1 convolution_convert_fusion.6
  314.4 2.1 copy.45
  316.6 8.7 %convolution_convert_fusion = bf16[1024,2048]{1,0:T(8,128)(2,1)} fusion(bf16[1024,1024]{1,0:T(8,128)(2,1)} %all-gather.7.cloned.1.call-done, bf16[1024,1024]{1,0:T(8,128)(2,1)S(1)} %copy-done.31, bf16[1024,1024]{1,0:T(8,128)(2,1)} %copy-done.58), kind=kOutput, calls=%fused_computation.74 | convolution fusion | flops 4305453056 | bytes 10485760 | tf_op jit(solution)/shard_map/sd,sc->dc/dot_general | solution.py:205
  326.4 3.1 convolution_convert_fusion.7
  329.6 122.0 %while.30 = (s32[]{:T(128)}, f32[4,1024,64]{1,2,0:T(8,128)}, f32[4,1024,64]{1,2,0:T(8,128)}, f32[2,4,512,64]{2,3,1,0:T(8,128)}, s32[2]{0:T(128)S(1)}, /*index=5*...) while((s32[]{:T(128)}, f32[4,1024,64]{1,2,0:T(8,128)}, ...), condition=%wide.region_19.20_spmd.clone.clone, body=%wide.region_17.19_spmd.clone.sunk.clone | while | flops 1399331328 | bytes 148969808 | solution.py:121
  333.7 1.4 fusion.195
  335.3 2.6 fusion.198
  339.5 4.6 fusion.194
  344.1 23.7 %fusion.197 = f32[4,1024,64]{1,2,0:T(8,128)} fusion(f32[4,512,1024]{2,1,0:T(8,128)} %fusion.194, f32[4,512,1024]{2,1,0:T(8,128)} %copy-done.2, f32[4,512]{1,0:T(4,128)S(1)} %dynamic-slice_bitcast_fusion.3, pred[512,1024]{1,0:T(8,128)(4,1)} %copy-done.18, f32[4,1024,64]{1,2,0:T(8,128)} %get-tuple-element.498, pred[]{:T(512)S(6)} %compare.8, ...), kind=kOutput, calls=%fused_computation.37.clone.1.clone | convolution fusion | flops 292031488 | bytes 36978692 | tf_op jit(solution)/shard_map/while/body/eval_jaxpr/hqk,hqd->hkd/dot_general | solution.py:108
  367.8 22.6 %fusion.199 = f32[2,4,512,64]{2,3,1,0:T(8,128)} fusion(f32[2,4,512,64]{2,3,1,0:T(8,128)} %get-tuple-element.500, s32[]{:T(128)S(6)} %copy.74, bf16[4,1024,64]{1,2,0:T(8,128)(2,1)S(1)} %get-tuple-element.515, f32[4,512,1024]{2,1,0:T(8,128)} %fusion.194, f32[4,512,1024]{2,1,0:T(8,128)} %copy-done.2, ...), kind=kOutput, calls=%fused_computation.40.clone.1.clone | convolution fusion | flops 291507200 | bytes 35667972 | tf_op jit(solution)/shard_map/while/body/eval_jaxpr/hqk,hkd->hqd/dot_general | solution.py:105
  394.3 1.4 fusion.195
  395.8 2.6 fusion.198
  400.0 4.6 fusion.194
  404.6 24.1 %fusion.197 = f32[4,1024,64]{1,2,0:T(8,128)} fusion(f32[4,512,1024]{2,1,0:T(8,128)} %fusion.194, f32[4,512,1024]{2,1,0:T(8,128)} %copy-done.2, f32[4,512]{1,0:T(4,128)S(1)} %dynamic-slice_bitcast_fusion.3, pred[512,1024]{1,0:T(8,128)(4,1)} %copy-done.18, f32[4,1024,64]{1,2,0:T(8,128)} %get-tuple-element.498, pred[]{:T(512)S(6)} %compare.8, ...), kind=kOutput, calls=%fused_computation.37.clone.1.clone | convolution fusion | flops 292031488 | bytes 36978692 | tf_op jit(solution)/shard_map/while/body/eval_jaxpr/hqk,hqd->hkd/dot_general | solution.py:108
  428.7 22.6 %fusion.199 = f32[2,4,512,64]{2,3,1,0:T(8,128)} fusion(f32[2,4,512,64]{2,3,1,0:T(8,128)} %get-tuple-element.500, s32[]{:T(128)S(6)} %copy.74, bf16[4,1024,64]{1,2,0:T(8,128)(2,1)S(1)} %get-tuple-element.515, f32[4,512,1024]{2,1,0:T(8,128)} %fusion.194, f32[4,512,1024]{2,1,0:T(8,128)} %copy-done.2, ...), kind=kOutput, calls=%fused_computation.40.clone.1.clone | convolution fusion | flops 291507200 | bytes 35667972 | tf_op jit(solution)/shard_map/while/body/eval_jaxpr/hqk,hkd->hqd/dot_general | solution.py:105
  451.6 1.4 copy.53
  454.5 1.8 fusion.91
  458.6 1.8 fusion.81
  460.4 1.6 copy.43
  462.1 4.6 convolution_convert_fusion.4
  472.2 21.6 %all-reduce.7 = (bf16[256]{0:T(256)(128)(2,1)S(1)}, bf16[1024]{0:T(1024)(128)(2,1)S(1)}, bf16[1024]{0:T(1024)(128)(2,1)S(1)}) all-reduce(bf16[256]{0:T(256)(128)(2,1)S(1)} %convert_element_type.174, bf16[1024]{0:T(1024)(128)(2,1)S(1)} %get-tuple-element.200, ...), channel_id=10, replica_groups=mesh['dp'=8,'mp'=4] {'dp'}, use_global_device_ids=true, to_apply=%region_29.30.clone | all-reduce | flops 2304 | bytes 9216
  495.6 15.1 %reduce-scatter.33.cloned.1.call-done = bf16[128,256]{1,0:T(8,128)(2,1)} async-done(((bf16[1024,256]{1,0:T(8,128)(2,1)}), bf16[128,256]{1,0:T(8,128)(2,1)}) %reduce-scatter.33.cloned.1.call-update) | async-done | bytes 65552
  512.3 89.4 %reduce-scatter.29.cloned.1.call-done = bf16[128,2048]{1,0:T(8,128)(2,1)} async-done(((bf16[1024,2048]{1,0:T(8,128)(2,1)}), bf16[128,2048]{1,0:T(8,128)(2,1)}) %reduce-scatter.29.cloned.1.call-update) | async-done | bytes 524304 | tf_op jit(solution)/shard_map/reduce_scatter | solution.py:254
  601.7 2.1 fusion.106
  603.8 65.9 %reduce-scatter.31.cloned.1.call-done = bf16[128,768]{1,0:T(8,128)(2,1)} async-done(((bf16[1024,768]{1,0:T(8,128)(2,1)}), bf16[128,768]{1,0:T(8,128)(2,1)}) %reduce-scatter.31.cloned.1.call-update) | async-done | bytes 196624
  673.1 29.5 %reduce-scatter.27.cloned.1.call-done = bf16[256,1024]{1,0:T(8,128)(2,1)} async-done(((bf16[1024,1024]{1,0:T(8,128)(2,1)}), bf16[256,1024]{1,0:T(8,128)(2,1)}) %reduce-scatter.27.cloned.1.call-update) | async-done | bytes 524304 | tf_op jit(solution)/shard_map/reduce_scatter | solution.py:230
  702.6 2.6 convert_add_fusion.1
  (240 shorter events, 46.9 us)
Async XLA Ops:
  7.2 137.9 %copy-start = (bf16[1024,1024]{1,0:T(8,128)(2,1)S(1)}, bf16[1024,1024]{1,0:T(8,128)(2,1)}, u32[]{:S(2)}) copy-start(bf16[1024,1024]{1,0:T(8,128)(2,1)} %param.29) | copy-start | bytes 6291460
  7.2 27.7 %all-gather.5.cloned.1.call-start = ((), (), s32[]{:S(2)}) async-start(), calls=%async_computation.10 | async-start | bytes 2621440 | tf_op jit(solution)/shard_map/all_gather | solution.py:150
  7.9 97.3 %reduce-scatter.21.cloned.1.call-start = ((), (), s32[]{:S(2)}) async-start(), calls=%async_computation.11 | async-start | bytes 2621440 | tf_op jit(solution)/shard_map/reduce_scatter | solution.py:167
  8.7 31.9 %copy-start.52 = (f32[4,64]{1,0:T(4,128)}, f32[4,64]{1,0:T(4,128)S(1)}, u32[]{:S(2)}) copy-start(f32[4,64]{1,0:T(4,128)S(1)} %mul.518) | copy-start | bytes 3076
  16.7 22.4 %copy-start.32 = (f32[1024,32]{0,1:T(8,128)}, f32[1024,32]{0,1:T(8,128)S(1)}, u32[]{:S(2)}) copy-start(f32[1024,32]{0,1:T(8,128)S(1)} %get-tuple-element.280) | copy-start | bytes 393220
  16.7 22.4 %copy-start.34 = (f32[1024,32]{0,1:T(8,128)}, f32[1024,32]{0,1:T(8,128)S(1)}, u32[]{:S(2)}) copy-start(f32[1024,32]{0,1:T(8,128)S(1)} %get-tuple-element.281) | copy-start | bytes 393220
  39.1 2.7 copy-start.38
  39.5 2.3 copy-start.12
  39.5 2.3 copy-start.14
  39.5 2.3 copy-start.16
  39.8 2.0 copy-start.42
  48.7 2.4 copy-start.25
  61.7 2.4 copy-start.25
  67.8 40.3 %copy-start.4 = (bf16[4,1024,64]{1,2,0:T(8,128)(2,1)}, bf16[4,1024,64]{1,2,0:T(8,128)(2,1)S(1)}, u32[]{:S(2)}) copy-start(bf16[4,1024,64]{1,2,0:T(8,128)(2,1)S(1)} %get-tuple-element.535) | copy-start | bytes 1572868
  67.8 38.6 %copy-start.46 = (f32[1024]{0:T(1024)S(1)}, f32[1024]{0:T(1024)}, u32[]{:S(2)}) copy-start(f32[1024]{0:T(1024)} %param.33) | copy-start | bytes 12292
  73.6 59.7 %all-gather.7.cloned.1.call-start = ((), (), s32[]{:S(2)}) async-start(), calls=%async_computation.12 | async-start | bytes 2621440 | tf_op jit(solution)/shard_map/all_gather | solution.py:175
  110.6 69.7 %reduce-scatter.23.cloned.1.call-start = ((), (), s32[]{:S(2)}) async-start(), calls=%async_computation.13 | async-start | bytes 2621440 | tf_op jit(solution)/shard_map/reduce_scatter | solution.py:182
  111.1 3.3 copy-start.24
  116.0 24.3 %copy-start.54 = (f32[1024]{0:T(1024)S(1)}, f32[1024]{0:T(1024)}, u32[]{:S(2)}) copy-start(f32[1024]{0:T(1024)} %param.32) | copy-start | bytes 12292
  116.0 24.3 %copy-start.55 = (f32[1024]{0:T(1024)S(1)}, f32[1024]{0:T(1024)}, u32[]{:S(2)}) copy-start(f32[1024]{0:T(1024)} %param.31) | copy-start | bytes 12292
  140.3 3.4 copy-start.21
  145.0 36.6 %copy-start.3 = (bf16[256,1024]{1,0:T(8,128)(2,1)S(1)}, bf16[256,1024]{1,0:T(8,128)(2,1)}, u32[]{:S(2)}) copy-start(bf16[256,1024]{1,0:T(8,128)(2,1)} %reduce-scatter.21.cloned.1.call-done) | copy-start | bytes 1572868
  145.0 36.6 %copy-start.51 = (f32[1024]{0:T(1024)S(1)}, f32[1024]{0:T(1024)}, u32[]{:S(2)}) copy-start(f32[1024]{0:T(1024)} %param.34) | copy-start | bytes 12292
  148.7 62.4 %all-gather.9.cloned.1.call-start = ((), (), s32[]{:S(2)}) async-start(), calls=%async_computation.14 | async-start | bytes 2621440 | tf_op jit(solution)/shard_map/all_gather | solution.py:190
  180.3 7.0 copy-start.19
  188.4 72.2 %reduce-scatter.25.cloned.1.call-start = ((), (), s32[]{:S(2)}) async-start(), calls=%async_computation.15 | async-start | bytes 2621440 | tf_op jit(solution)/shard_map/reduce_scatter | solution.py:197
  220.9 39.7 %copy-start.7 = (bf16[256,1024]{1,0:T(8,128)(2,1)S(1)}, bf16[256,1024]{1,0:T(8,128)(2,1)}, u32[]{:S(2)}) copy-start(bf16[256,1024]{1,0:T(8,128)(2,1)} %param.20) | copy-start | bytes 1572868
  220.9 39.7 %copy-start.9 = (f32[256,1024]{1,0:T(8,128)S(1)}, f32[256,1024]{1,0:T(8,128)}, u32[]{:S(2)}) copy-start(f32[256,1024]{1,0:T(8,128)} %copy-done.8) | copy-start | bytes 3145732
  220.9 39.7 %copy-start.20 = (bf16[256,1024]{1,0:T(8,128)(2,1)S(1)}, bf16[256,1024]{1,0:T(8,128)(2,1)}, u32[]{:S(2)}) copy-start(bf16[256,1024]{1,0:T(8,128)(2,1)} %reduce-scatter.23.cloned.1.call-done) | copy-start | bytes 1572868
  229.0 57.6 %reduce-scatter.37.cloned.1.call-start = ((), (), s32[]{:S(2)}) async-start(), calls=%async_computation.22 | async-start | bytes 327680
  266.4 45.0 %all-gather.11.cloned.1.call-start = ((), (), s32[]{:S(2)}) async-start(), calls=%async_computation.16 | async-start | bytes 2621440 | tf_op jit(solution)/shard_map/all_gather | solution.py:210
  268.7 199.9 %reduce-scatter.35.cloned.1.call-start = ((), (), s32[]{:S(2)}) async-start(), calls=%async_computation.21 | async-start | bytes 2359296
  273.4 37.9 %copy-start.28 = (bf16[32,8,2,512]{3,1,2,0:T(8,128)(2,1)S(1)}, bf16[32,8,2,512]{3,1,2,0:T(8,128)(2,1)}, u32[]{:S(2)}) copy-start(bf16[32,8,2,512]{3,1,2,0:T(8,128)(2,1)} %copy-done.27) | copy-start | bytes 1572868
  276.0 40.5 %copy-start.31 = (bf16[1024,1024]{1,0:T(8,128)(2,1)S(1)}, bf16[1024,1024]{1,0:T(8,128)(2,1)}, u32[]{:S(2)}) copy-start(bf16[1024,1024]{1,0:T(8,128)(2,1)} %copy-done.30) | copy-start | bytes 6291460
  276.1 194.7 %reduce-scatter.39.cloned.1.call-start = ((), (), s32[]{:S(2)}) async-start(), calls=%async_computation.23 | async-start | bytes 73728
  286.6 224.1 %reduce-scatter.33.cloned.1.call-start = ((), (), s32[]{:S(2)}) async-start(), calls=%async_computation.20 | async-start | bytes 589824
  316.5 285.2 %reduce-scatter.29.cloned.1.call-start = ((), (), s32[]{:S(2)}) async-start(), calls=%async_computation.18 | async-start | bytes 4718592 | tf_op jit(solution)/shard_map/reduce_scatter | solution.py:254
  325.3 4.2 copy-start.5
  325.3 4.2 copy-start.6
  325.4 344.3 %reduce-scatter.31.cloned.1.call-start = ((), (), s32[]{:S(2)}) async-start(), calls=%async_computation.19 | async-start | bytes 1769472
  329.5 124.9 %copy-start.11 = (f32[1024,4,32]{0,2,1:T(8,128)S(1)}, f32[1024,4,32]{0,2,1:T(8,128)}, u32[]{:S(2)}) copy-start(f32[1024,4,32]{0,2,1:T(8,128)} %copy-done.10) | copy-start | bytes 1572868
  329.5 124.9 %copy-start.13 = (f32[1024,4,32]{0,2,1:T(8,128)S(1)}, f32[1024,4,32]{0,2,1:T(8,128)}, u32[]{:S(2)}) copy-start(f32[1024,4,32]{0,2,1:T(8,128)} %copy-done.12) | copy-start | bytes 1572868
  329.5 124.9 %copy-start.15 = (f32[1024,4,32]{0,2,1:T(8,128)S(1)}, f32[1024,4,32]{0,2,1:T(8,128)}, u32[]{:S(2)}) copy-start(f32[1024,4,32]{0,2,1:T(8,128)} %copy-done.14) | copy-start | bytes 1572868
  329.5 124.9 %copy-start.43 = (f32[1024,4]{0,1:T(4,128)S(1)}, f32[1024,4]{0,1:T(4,128)}, u32[]{:S(2)}) copy-start(f32[1024,4]{0,1:T(4,128)} %copy-done.42) | copy-start | bytes 49156
  329.5 124.9 %copy-start.45 = (f32[1024,4]{0,1:T(4,128)S(1)}, f32[1024,4]{0,1:T(4,128)}, u32[]{:S(2)}) copy-start(f32[1024,4]{0,1:T(4,128)} %copy-done.44) | copy-start | bytes 49156
  329.5 124.9 %copy-start.53 = (f32[4,64]{1,0:T(4,128)S(1)}, f32[4,64]{1,0:T(4,128)}, u32[]{:S(2)}) copy-start(f32[4,64]{1,0:T(4,128)} %copy-done.52) | copy-start | bytes 3076
  333.6 1.4 copy-start.18
  333.7 1.4 copy-start.23
  333.7 1.6 copy-start.36
  335.3 3.3 copy-start.2
  394.3 1.4 copy-start.18
  394.3 1.4 copy-start.23
  394.3 1.6 copy-start.36
  395.8 3.3 copy-start.2
  451.6 2.9 copy-start.22
  451.6 4.7 copy-start.50
  451.6 4.7 copy-start.48
  451.6 4.7 copy-start.17
  454.4 3.3 copy-start.39
  457.0 1.6 copy-start.56
  460.4 1.7 copy-start.40
  462.0 4.7 copy-start.57
  462.1 240.5 %reduce-scatter.27.cloned.1.call-start = ((), (), s32[]{:S(2)}) async-start(), calls=%async_computation.17 | async-start | bytes 2621440 | tf_op jit(solution)/shard_map/reduce_scatter | solution.py:230
  468.7 236.5 %copy-start.1 = (bf16[1024,1024]{1,0:T(8,128)(2,1)S(1)}, bf16[1024,1024]{1,0:T(8,128)(2,1)}, u32[]{:S(2)}) copy-start(bf16[1024,1024]{1,0:T(8,128)(2,1)} %param.29) | copy-start | bytes 6291460
  (16 other events, 16.2 us)
Sparse Core Ops, SparseCore 0:
  9.6 25.2 all-gather.4
  73.8 31.4 reduce-scatter.20
  110.7 22.5 all-gather.6
  148.8 31.3 reduce-scatter.22
  188.5 22.5 all-gather.8
  229.1 31.4 reduce-scatter.24
  266.5 20.0 reduce-scatter.36
  288.7 22.5 all-gather.10
  314.9 67.8 reduce-scatter.34
  386.0 60.2 reduce-scatter.38
  449.6 61.0 reduce-scatter.32
  514.6 87.0 reduce-scatter.28
  605.1 64.5 reduce-scatter.30
  672.2 30.3 reduce-scatter.26
where the time goes:
time: 721 us; the launch traced here: 712 us
  waiting for transfers between devices  389 us (54%)
  matrix products  182 us (25%)
  local copies, waits for them, and re-layouts  49.2 us (7%)
  other arithmetic  45 us (6%)
  blocking collectives  21.6 us (3%)
  between operations  16.5 us (2%)
  loops' own time  8.5 us (1%)
    unnamed x19, waiting for transfers between devices  92.4 us
    reduce_scatter x1, waiting for transfers between devices, body(): lax.psum_scatter(grad_w_pair.astype(jnp.bfloat16), 'dp', scatter_dimensio...  89.4 us
    dot_general x2, matrix products, one_block(): jnp.einsum('hqk,hqd->hkd', grad_scores, query_block, preferred_element_ty...  47.8 us
    dot_general x2, matrix products, one_block(): jnp.einsum('hqk,hkd->hqd', grad_scores, key_heads, preferred_element_type...  45.2 us
    reduce_scatter x1, waiting for transfers between devices, body(): lax.psum_scatter(jnp.dot(attended_low, w_out, preferred_element_type=jnp....  31.5 us
    reduce_scatter x1, waiting for transfers between devices, body(): lax.psum_scatter(jnp.dot(inner_low, w_down, preferred_element_type=jnp.fl...  31.5 us
    reduce_scatter x1, waiting for transfers between devices, body(): lax.psum_scatter(jnp.einsum('sc,dc->sd', grad_pair, w_pair, preferred_ele...  31.4 us
    unnamed x120, local copies, waits for them, and re-layouts  30.9 us
  transfers between devices with their start and end apart: 14, of which 12 were waited for; matrix products, arithmetic and copies ran while one was open for 25% of the time, Pallas kernels for 0%

commit v1 on v0

v1 whole, which is shorter than its diff:
```python
from functools import partial

import jax
import jax.numpy as jnp
from jax import lax
from jax.experimental import pallas as pl
from jax.experimental.layout import Layout, with_layout_constraint
from jax.experimental.pallas import tpu as pltpu
from jax.sharding import PartitionSpec as P

HEAD_DIM = 64
HALF = HEAD_DIM // 2
BLOCK = 256
EPSILON = 1e-06
LOG2E = 1.4426950408889634
FILL = 20_000_000_000
BF = jnp.bfloat16
F32 = jnp.float32


def swap(value, bit, size, name="mp"):
    return lax.ppermute(value, name, [(i, i ^ bit) for i in range(size)])


def gather_start(own, size):
    blocks = {0: own}
    bit = size // 2
    while bit > 1:
        blocks.update({b ^ bit: swap(v, bit, size) for b, v in list(blocks.items())})
        bit //= 2
    return {b: v for b, v in blocks.items() if b}


def gather_finish(blocks, done, size, order=None, own=None):
    if order is not None:
        blocks = {b: order.fill(own, v) for b, v in blocks.items()}
    blocks = {b: after(v, done) for b, v in blocks.items()}
    for b, v in list(blocks.items()):
        got = swap(v, 1, size)
        blocks[b ^ 1] = got if order is None else order.fill(v, got)
    return [blocks[b] for b in range(2, size)]


def add_low(left, right):
    return (left.astype(F32) + right.astype(F32)).astype(BF)


def scatter_far(far, size, order=None):
    sums = {}
    for b in range(size - 2, 1, -2):
        got = swap(far[b - 1], 1, size)
        if order is not None:
            got = order.fill(far[b - 1], got)
        sums[b] = add_low(far[b - 2], got)
    terms = []
    bit = 2
    while bit < size:
        kept = {}
        for b in sorted(sums, reverse=True):
            if not b & bit:
                kept[b] = add_low(sums[b], swap(sums[b ^ bit], bit, size))
            elif b == bit:
                sent = sums[b]
                terms.append(swap(sent, bit, size))
        sums = kept
        bit *= 2
    return terms, sent


def after(value, done):
    return lax.optimization_barrier((value, done))[0]


def stand_in_kernel(mark_ref, sent_ref, out_ref):
    out_ref[...] = mark_ref[...]


class Order:
    def __init__(self):
        self.last = None
        self.hint = jnp.zeros((8, 128), F32)

    def fill(self, sent, *got):
        tile = pl.BlockSpec((8, 128), lambda i: (0, 0))
        hint = pl.pallas_call(
            stand_in_kernel,
            grid=(1,),
            in_specs=[tile, pl.BlockSpec(memory_space=pl.ANY)],
            out_specs=tile,
            out_shape=jax.ShapeDtypeStruct((8, 128), F32),
            cost_estimate=pl.CostEstimate(flops=FILL, bytes_accessed=0, transcendentals=0),
            name="stand_in",
        )(self.hint, sent)
        *got, self.hint = lax.optimization_barrier((*got, hint))
        return got if len(got) > 1 else got[0]

    def tie(self, *values):
        if self.last is not None:
            values = lax.optimization_barrier((*values, self.last))[:-1]
        return values if len(values) > 1 else values[0]

    def mark(self, value):
        self.last = value
        return value


def take(rows, place, bits, left, other):
    at = (place // bits[0]) % 2
    lead = 1 << left.index(bits[0])
    split = rows.reshape(lead, 2, rows.shape[0] // (2 * lead), rows.shape[1])
    half = lax.dynamic_slice_in_dim(split, 1 - at if other else at, 1, 1)
    return half.reshape(rows.shape[0] // 2, rows.shape[1])


class Reduction:
    def __init__(self, order, grad, bits, place):
        self.order, self.bits, self.place = order, list(bits), place
        self.size = 1 << len(bits)
        self.left = [1 << i for i in reversed(range(len(bits)))]
        self.send([grad])

    def send(self, terms):
        sides = []
        for other in (True, False):
            halves = [take(t, self.place, self.bits, self.left, other) for t in terms]
            sides.append(halves[0] if len(halves) == 1 else add_low(*halves))
        self.held = sides[1]
        self.got = swap(self.order.mark(sides[0]), self.bits[0], self.size, "dp")
        self.left.remove(self.bits.pop(0))

    def step(self):
        held, got = self.order.tie(self.held, self.got)
        if self.bits:
            self.send([held, got])
        else:
            return self.order.mark(held.astype(F32) + got.astype(F32))


VMEM_LIMIT = 56 * 1024 * 1024


def whole_spec(shape):
    return pl.BlockSpec(shape, lambda *_: (0,) * len(shape))


def dot(left, right):
    return jnp.dot(left, right, preferred_element_type=F32)


def dot_tn(left, right):
    return lax.dot_general(left, right, (((0,), (0,)), ((), ())), preferred_element_type=F32)


def dot_nt(left, right):
    return lax.dot_general(left, right, (((1,), (1,)), ((), ())), preferred_element_type=F32)


def cost(*_):
    return pl.CostEstimate(flops=1, bytes_accessed=1, transcendentals=0)


def params():
    return pltpu.CompilerParams(vmem_limit_bytes=VMEM_LIMIT)


def project_kernel(first, count, me_ref, *refs):
    x_refs, refs = refs[:count], refs[count:]
    wq_ref, wk_ref, wv_ref, cos_ref, sin_ref, scale_ref = refs[:6]
    q_ref, k_ref, v_ref, rq_ref, rk_ref = refs[-5:]
    width = q_ref.shape[0]
    heads = width // HEAD_DIM
    scale = scale_ref[...].reshape(heads, 2, HALF, 1)
    for b in range(count):
        here = slice(b * BLOCK, (b + 1) * BLOCK)
        x = x_refs[b][...]
        at = pl.ds(pl.multiple_of((me_ref[0] ^ (first + b)) * BLOCK, BLOCK), BLOCK)
        cos, sin = cos_ref[:, at][None], sin_ref[:, at][None]
        for w_ref, o_ref, r_ref in ((wq_ref, q_ref, rq_ref), (wk_ref, k_ref, rk_ref)):
            pairs = dot(x, w_ref[...]).T.reshape(heads, 2, HALF, BLOCK)
            one, two = pairs[:, 0], pairs[:, 1]
            ra, rb = one * cos - two * sin, two * cos + one * sin
            square = jnp.sum(ra * ra + rb * rb, axis=1, keepdims=True) * (1.0 / HEAD_DIM)
            r = lax.rsqrt(square + EPSILON)
            r_ref[:, :, here] = r
            out = jnp.stack([ra * r * scale[:, 0], rb * r * scale[:, 1]], axis=1)
            o_ref[:, here] = out.reshape(width, BLOCK).astype(BF)
        v_ref[:, here] = dot(x, wv_ref[...]).T.astype(BF)


def project(me, first, blocks, held, wq, wk, wv, cos, sin, scale):
    count = len(blocks)
    seq = cos.shape[1]
    depth, width = wq.shape
    heads = width // HEAD_DIM
    place = first // count
    tall = pl.BlockSpec((width, count * BLOCK), lambda i, me: (0, place))
    row = pl.BlockSpec((heads, 1, count * BLOCK), lambda i, me: (0, 0, place))
    held = list(held)
    return pl.pallas_call(
        partial(project_kernel, first, count),
        grid_spec=pltpu.PrefetchScalarGridSpec(
            num_scalar_prefetch=1,
            grid=(1,),
            in_specs=[whole_spec((BLOCK, depth))] * count
            + [whole_spec((depth, width))] * 3
            + [whole_spec((HALF, seq))] * 2
            + [whole_spec((width, 1))]
            + [pl.BlockSpec(memory_space=pl.ANY)] * len(held),
            out_specs=[tall, tall, tall, row, row],
        ),
        out_shape=[jax.ShapeDtypeStruct((width, seq), BF)] * 3
        + [jax.ShapeDtypeStruct((heads, 1, seq), F32)] * 2,
        input_output_aliases={count + 7 + i: i for i in range(len(held))},
        compiler_params=params(),
        cost_estimate=cost(6 * count * BLOCK * depth * width, 2 * count * BLOCK * depth + 6 * depth * width),
        name="project",
    )(me, *blocks, wq, wk, wv, cos, sin, scale, *held)


def block_at(me, index):
    return pl.ds(pl.multiple_of((me ^ index) * BLOCK, BLOCK), BLOCK)


def allowed(start, low, first, diagonal):
    key = lax.broadcasted_iota(jnp.int32, (BLOCK, BLOCK), 0)
    seen = key >= start - first
    if diagonal:
        seen = seen & (key <= lax.broadcasted_iota(jnp.int32, (BLOCK, BLOCK), 1))
    return seen


def attend_kernel(me_ref, q_ref, k_ref, v_ref, start_ref, o_ref, l_ref, kn_ref):
    me = me_ref[0]
    blocks = q_ref.shape[1] // BLOCK
    factor = LOG2E / HEAD_DIM**0.5
    for j in range(blocks):
        kn_ref[j * BLOCK : (j + 1) * BLOCK, :] = k_ref[:, block_at(me, j)].T
    for i in range(blocks):
        here = block_at(me, i)
        q = q_ref[:, here]
        start = start_ref[:, i * BLOCK : (i + 1) * BLOCK]
        total = jnp.zeros((1, BLOCK), F32)
        out = jnp.zeros((HEAD_DIM, BLOCK), F32)
        for j in range(i + 1):
            s = jnp.dot(kn_ref[j * BLOCK : (j + 1) * BLOCK, :], q, preferred_element_type=F32)
            p = jnp.where(allowed(start, i, j * BLOCK, i == j), jnp.exp2(s * factor), 0.0)
            total = total + jnp.sum(p, axis=0, keepdims=True)
            out = out + jnp.dot(v_ref[:, block_at(me, j)], p.astype(BF), preferred_element_type=F32)
        o_ref[:, here] = (out / total).astype(BF)
        l_ref[0, :, here] = jnp.log2(total)


def attend(me, q, k, v, start):
    width, seq = q.shape
    heads = width // HEAD_DIM
    head = pl.BlockSpec((HEAD_DIM, seq), lambda h, me: (h, 0))
    row = pl.BlockSpec((1, 1, seq), lambda h, me: (h, 0, 0))
    return pl.pallas_call(
        attend_kernel,
        grid_spec=pltpu.PrefetchScalarGridSpec(
            num_scalar_prefetch=1,
            grid=(heads,),
            in_specs=[head, head, head, pl.BlockSpec((1, seq), lambda h, me: (0, 0))],
            out_specs=[head, row],
            scratch_shapes=[pltpu.VMEM((seq, HEAD_DIM), BF)],
        ),
        out_shape=[
            jax.ShapeDtypeStruct((width, seq), BF),
            jax.ShapeDtypeStruct((heads, 1, seq), F32),
        ],
        cost_estimate=pl.CostEstimate(
            flops=8 * seq * seq * width, bytes_accessed=8 * seq * width, transcendentals=heads * seq * seq // 2
        ),
        compiler_params=params(),
        name="attend",
    )(me, q, k, v, start)


PAIR = 2 * HEAD_DIM


def attend_back_kernel(
    me_ref, q_ref, k_ref, v_ref, o_ref, do_ref, l_ref, start_ref, rq_ref, rk_ref, cos_ref, sin_ref, scale_ref,
    g_ref, gs_ref, qn_ref, kn_ref, vn_ref, dn_ref, dq_ref,
):
    me = me_ref[0]
    blocks = q_ref.shape[1] // BLOCK
    factor = LOG2E / HEAD_DIM**0.5
    scale = scale_ref[...]

    def rows(j):
        return slice(j * BLOCK, (j + 1) * BLOCK)

    for j in range(blocks):
        here = block_at(me, j)
        qn_ref[rows(j), :] = q_ref[:, here].T
        kn_ref[rows(j), :] = k_ref[:, here].T
        vn_ref[rows(j), :] = v_ref[:, here].T
        dn_ref[rows(j), :] = do_ref[:, here].T

    def prepare_back(grad, value, r_ref, j):
        at = block_at(me, j)
        unit = value.astype(F32) / scale
        grad = grad * (1.0 / HEAD_DIM**0.5)
        share = jnp.sum(unit * grad, axis=1, keepdims=True)
        g = grad * scale
        cos, sin = cos_ref[:, rows(j)], sin_ref[:, rows(j)]
        out = []
        for h in range(2):
            head = slice(h * HEAD_DIM, (h + 1) * HEAD_DIM)
            inner = jnp.sum(unit[head] * g[head], axis=0, keepdims=True) * (1.0 / HEAD_DIM)
            part = (g[head] - unit[head] * inner) * r_ref[h, :, at]
            one, two = part[:HALF], part[HALF:]
            out += [one * cos + two * sin, two * cos - one * sin]
        return jnp.concatenate(out, axis=0).T.astype(BF), share

    total_share = jnp.zeros((PAIR, 1), F32)
    for j in range(blocks):
        at_j = block_at(me, j)
        dks, dvs = [], []
        for h in range(2):
            head = slice(h * HEAD_DIM, (h + 1) * HEAD_DIM)
            kn, vn, kt = kn_ref[rows(j), head], vn_ref[rows(j), head], k_ref[head, at_j]
            dk = jnp.zeros((BLOCK, HEAD_DIM), F32)
            dv = jnp.zeros((BLOCK, HEAD_DIM), F32)
            for i in range(j, blocks):
                at_i = block_at(me, i)
                do = do_ref[head, at_i]
                delta = jnp.sum(do.astype(F32) * o_ref[head, at_i].astype(F32), axis=0, keepdims=True)
                s = dot(kn, q_ref[head, at_i])
                p = jnp.exp2(s * factor - l_ref[h, :, at_i])
                p = jnp.where(allowed(start_ref[:, rows(i)], i, j * BLOCK, i == j), p, 0.0)
                ds = (p * (dot(vn, do) - delta)).astype(BF)
                dv = dv + dot(p.astype(BF), dn_ref[rows(i), head])
                dk = dk + dot(ds, qn_ref[rows(i), head])
                dq = dot(kt, ds)
                if j == 0:
                    dq_ref[head, rows(i)] = dq
                else:
                    dq_ref[head, rows(i)] += dq
            dks.append(dk)
            dvs.append(dv)
        g_ref[at_j, 2 * PAIR :] = jnp.concatenate(dvs, axis=1).astype(BF)
        out, share = prepare_back(jnp.concatenate(dks, axis=1).T, k_ref[:, at_j], rk_ref, j)
        g_ref[at_j, PAIR : 2 * PAIR] = out
        total_share = total_share + share
        out, share = prepare_back(dq_ref[:, rows(j)], q_ref[:, at_j], rq_ref, j)
        g_ref[at_j, :PAIR] = out
        total_share = total_share + share
    gs_ref[...] = total_share


def attend_back(which, me, q, k, v, o, do, l, start, rq, rk, cos, sin, scale):
    seq = q.shape[1]
    pair = pl.BlockSpec((PAIR, seq), lambda i, me: (which, 0))
    row = pl.BlockSpec((2, 1, seq), lambda i, me: (which, 0, 0))
    return pl.pallas_call(
        attend_back_kernel,
        grid_spec=pltpu.PrefetchScalarGridSpec(
            num_scalar_prefetch=1,
            grid=(1,),
            in_specs=[pair] * 5
            + [row, whole_spec((1, seq)), row, row, whole_spec((HALF, seq)), whole_spec((HALF, seq))]
            + [pl.BlockSpec((PAIR, 1), lambda i, me: (which, 0))],
            out_specs=[whole_spec((seq, 3 * PAIR)), whole_spec((PAIR, 1))],
            scratch_shapes=[pltpu.VMEM((seq, PAIR), BF)] * 4 + [pltpu.VMEM((PAIR, seq), F32)],
        ),
        out_shape=[jax.ShapeDtypeStruct((seq, 3 * PAIR), BF), jax.ShapeDtypeStruct((PAIR, 1), F32)],
        compiler_params=params(),
        cost_estimate=cost(20 * seq * seq * PAIR, 16 * seq * PAIR, seq * seq),
        name="attend_back",
    )(me, q, k, v, o, do, l, start, rq, rk, cos, sin, scale)


def root_mean(values):
    return lax.rsqrt(jnp.mean(values * values, axis=-1, keepdims=True) + EPSILON)


def sum_refs(refs):
    total = refs[0][...].astype(F32)
    for ref in refs[1:]:
        total = total + ref[...].astype(F32)
    return total


def row_call(kernel, name, blocks, vectors, outs):
    depth = blocks[0].shape[1]
    return pl.pallas_call(
        kernel,
        grid=(1,),
        in_specs=[whole_spec((BLOCK, depth))] * len(blocks) + [whole_spec(t.shape) for t in vectors],
        out_specs=[whole_spec((rows, depth)) for _, rows in outs],
        out_shape=[jax.ShapeDtypeStruct((rows, depth), t) for t, rows in outs],
        compiler_params=params(),
        cost_estimate=cost(),
        name=name,
    )(*blocks, *vectors)


def middle_update(terms, x, alpha):
    n = len(terms)

    def kernel(*refs):
        x_ref, alpha_ref, mid_ref, low_ref = refs[n:]
        mixed = sum_refs(refs[:n])
        x = x_ref[...].astype(F32)
        stepped = x + alpha_ref[...] * (mixed * root_mean(mixed) - x)
        middle = stepped * root_mean(stepped)
        mid_ref[...] = middle
        low_ref[...] = middle.astype(BF)

    return row_call(kernel, "middle_update", [*terms, x], [alpha], [(F32, BLOCK), (BF, BLOCK)])


def step_back(base, mixed, alpha, grad):
    r_mixed = root_mean(mixed)
    unit = mixed * r_mixed
    apart = unit - base
    stepped = base + alpha * apart
    r = root_mean(stepped)
    value = stepped * r
    grad_step = r * (grad - value * jnp.mean(value * grad, axis=-1, keepdims=True))
    grad_unit = alpha * grad_step
    grad_mixed = r_mixed * (grad_unit - unit * jnp.mean(unit * grad_unit, axis=-1, keepdims=True))
    share = jnp.sum(grad_step * apart, axis=0, keepdims=True)
    return value, grad_step - grad_unit, grad_mixed, share


def last_update(terms, middle, cotangent, alpha):
    n = len(terms)

    def kernel(*refs):
        mid_ref, cot_ref, alpha_ref, out_ref, res_ref, low_ref, share_ref = refs[n:]
        value, res, grad_mixed, share = step_back(
            mid_ref[...], sum_refs(refs[:n]), alpha_ref[...], cot_ref[...].astype(F32)
        )
        out_ref[...] = value.astype(BF)
        res_ref[...] = res
        low_ref[...] = grad_mixed.astype(BF)
        share_ref[...] = share

    return row_call(kernel, "last_update", [*terms, middle, cotangent], [alpha], [(BF, BLOCK), (F32, BLOCK), (BF, BLOCK), (F32, 1)])


def input_update(terms, grad, hint):
    n = len(terms)

    def kernel(*refs):
        grad_ref, hint_ref, out_ref = refs[n:]
        out_ref[...] = sum_refs(refs[:n]) + grad_ref[...]

    return row_call(kernel, "input_update", [*terms, grad], [hint], [(F32, BLOCK)])[0]


def middle_back(terms, x, grads, grad_res, alpha):
    n, m = len(terms), len(grads)

    def kernel(*refs):
        x_ref, res_ref, alpha_ref, out_ref, low_ref, share_ref = refs[n + m :]
        grad = sum_refs(refs[n : n + m]) + res_ref[...]
        _, res, grad_mixed, share = step_back(
            x_ref[...].astype(F32), sum_refs(refs[:n]), alpha_ref[...], grad
        )
        out_ref[...] = res
        low_ref[...] = grad_mixed.astype(BF)
        share_ref[...] = share

    return row_call(kernel, "middle_back", [*terms, *grads, x, grad_res], [alpha], [(F32, BLOCK), (BF, BLOCK), (F32, 1)])


def body(
    n_mp, x_bits, z_bits,
    hidden_in, doc_index, doc_position, w_query, w_key, w_value, w_out, w_up, w_gate, w_down,
    score_scale, up_scale, gate_scale, alpha_attention, alpha_feedforward, cotangent,
):
    depth, width = w_query.shape
    seq = doc_position.shape[0]
    me = lax.axis_index("mp").astype(jnp.int32).reshape(1)
    place = lax.axis_index("dp").astype(jnp.int32)
    x_first = x_bits + z_bits
    z_first = z_bits[:1] + x_bits + z_bits[1:]
    n_dp = 1 << len(x_first)

    tokens = jnp.arange(seq, dtype=jnp.int32)
    start = (tokens - doc_position).reshape(1, seq)
    steps = jnp.arange(HALF).astype(F32)
    inverse = jnp.exp(steps * (-2.0 * jnp.log(10000.0) / HEAD_DIM))
    angles = inverse[:, None] * doc_position.astype(F32)[None, :]
    cos, sin = jnp.cos(angles), jnp.sin(angles)
    scale = score_scale.reshape(width, 1)
    alpha_attention = alpha_attention.reshape(1, depth)
    alpha_feedforward = alpha_feedforward.reshape(1, depth)
    up_scale, gate_scale = up_scale.reshape(1, -1), gate_scale.reshape(1, -1)
    far_count = n_mp - 2

    def join(blocks):
        return jnp.concatenate(blocks, axis=0)

    def cut(parts):
        return [parts[b * BLOCK : (b + 1) * BLOCK] for b in range(parts.shape[0] // BLOCK)]

    near = slice(0, 2 * BLOCK)
    rest = slice(2 * BLOCK, None)
    pairs = range(width // PAIR)

    def columns(w, i):
        return w[:, i * PAIR : (i + 1) * PAIR]

    w_pairs = [jnp.concatenate([columns(w, i) for w in (w_query, w_key, w_value)], axis=1) for i in pairs]

    coming = gather_start(hidden_in, n_mp)
    x_near = [hidden_in, swap(hidden_in, 1, n_mp)]
    held = project(me, 0, x_near, [], w_query, w_key, w_value, cos, sin, scale)
    x_far = gather_finish(coming, held[0], n_mp)
    for i in range(0, far_count, 2):
        held = project(me, 2 + i, x_far[i : i + 2], held, w_query, w_key, w_value, cos, sin, scale)
    q, k, v, rq, rk = held
    o, l = attend(me, q, k, v, start)
    far_terms, sent = scatter_far(cut(dot_tn(o[:, rest], w_out).astype(BF)), n_mp)
    parts = cut(dot_tn(after(o, sent)[:, near], w_out).astype(BF))
    attn_terms = [parts[0], swap(parts[1], 1, n_mp), *far_terms]
    middle, middle_low = middle_update(attn_terms, hidden_in, alpha_attention)

    def unit(rows):
        u = dot(rows, w_up)
        g = dot(rows, w_gate)
        gate = g * gate_scale
        inner = (u * up_scale * (gate / (1.0 + jnp.exp(-gate)))).astype(BF)
        return u.astype(BF), g.astype(BF), inner, dot(inner, w_down).astype(BF)

    coming = gather_start(middle_low, n_mp)
    mid_near = join([middle_low, swap(middle_low, 1, n_mp)])
    u0, g0, inner0, parts = unit(mid_near)
    mid_far = join(gather_finish(coming, parts, n_mp))
    u1, g1, inner1, far = unit(mid_far)
    far_terms, sent = scatter_far(cut(far), n_mp)
    parts = cut(after(parts, sent))
    mid_all, inner_all, x_all = lax.optimization_barrier(
        tuple(jnp.concatenate(t, axis=0) for t in ([mid_near, after(mid_far, sent)], [inner0, inner1], x_near + x_far))
    )
    ff_terms = [parts[0], swap(parts[1], 1, n_mp), *far_terms]
    layer_out, grad_res, grad_low, share_ff = last_update(ff_terms, middle, cotangent, alpha_feedforward)

    def unit_back(rows, u, g):
        grad = dot_nt(rows, w_down)
        u, g = u.astype(F32), g.astype(F32)
        gate = g * gate_scale
        sig = 1.0 / (1.0 + jnp.exp(-gate))
        by_up = grad * (gate * sig)
        by_gate = grad * (u * up_scale) * (sig * (1.0 + gate * (1.0 - sig)))
        du, dg = (by_up * up_scale).astype(BF), (by_gate * gate_scale).astype(BF)
        shares = jnp.stack([jnp.sum(by_up * u, axis=0), jnp.sum(by_gate * g, axis=0)])
        return du, dg, shares

    def unit_parts(du, dg):
        return (dot_nt(du, w_up) + dot_nt(dg, w_gate)).astype(BF)

    order = Order()
    coming = gather_start(grad_low, n_mp)
    g_near = [grad_low, swap(grad_low, 1, n_mp)]
    du0, dg0, shares0 = unit_back(join(g_near), u0, g0)
    near_parts = order.mark(unit_parts(du0, dg0))
    g_far = gather_finish(coming, near_parts, n_mp)
    g_all = join(g_near + g_far)
    grad_down = Reduction(order, dot_tn(g_all, inner_all).astype(BF), x_first, place)
    du1, dg1, shares1 = unit_back(order.tie(g_all)[2 * BLOCK :], u1, g1)
    far = unit_parts(du1, dg1)
    far_terms, sent = scatter_far(cut(far), n_mp, order)
    order.mark(sent)
    unit_scales = shares0 + shares1

    def over_tokens(near, far):
        return dot_tn(mid_all, jnp.concatenate([near, order.tie(far)], axis=0)).astype(BF)

    grad_gate = Reduction(order, over_tokens(dg0, dg1), z_first, place)
    grad_up = Reduction(order, over_tokens(du0, du1), x_first, place)
    parts = cut(order.tie(near_parts))
    mid_terms = [parts[0], swap(parts[1], 1, n_mp), *far_terms]
    mid_terms[-1] = order.fill(sent, order.tie(mid_terms[-1]))
    grad_x, grad_low, share_attn = middle_back(attn_terms, hidden_in, mid_terms, grad_res, alpha_attention)
    order.mark(grad_low)

    coming = gather_start(grad_low, n_mp)
    a_near = [grad_low, swap(grad_low, 1, n_mp)]
    do_near = order.mark(dot_nt(w_out, order.tie(join(a_near))).astype(BF))
    grad_down.step()
    a_far = gather_finish(coming, order.last, n_mp, order, grad_low)
    do = order.mark(jnp.concatenate([do_near, dot_nt(w_out, join(a_far)).astype(BF)], axis=1))
    a_all = join(a_near + a_far)
    grad_gate.step()
    grad_up.step()

    def rows_first(grad):
        return with_layout_constraint(grad.astype(BF), Layout(major_to_minor=(0, 1)))

    shares = jnp.concatenate([share_attn, share_ff], axis=0).reshape(2, n_mp, -1)
    shares = [lax.dynamic_index_in_dim(shares, me[0] ^ b, 1, keepdims=False).astype(BF) for b in range(n_mp)]
    alpha = [shares[0], swap(shares[1], 1, n_mp)]
    far_shares = [swap(t, 1, n_mp) if b % 2 else t for b, t in enumerate(shares[2:])]
    g_pairs, s_pairs, joints = [], [], []

    def rows_first(grad):
        return with_layout_constraint(grad.astype(BF), Layout(major_to_minor=(0, 1)))

    for i in pairs:
        g_pair, s_pair = attend_back(i, me, q, k, v, o, order.tie(do), l, start, rq, rk, cos, sin, scale)
        order.mark(g_pair)
        g_pairs.append(g_pair)
        s_pairs.append(s_pair)
        if i == 0:
            far_shares = order.tie(*far_shares, *alpha)
            alpha, far_shares = list(far_shares[-2:]), far_shares[:-2]
            far_shares = [add_low(*far_shares[b : b + 2]) for b in range(0, far_count, 2)]
            sums = {2 * b + 2: t for b, t in enumerate(far_shares)}
            bit = 2
            while bit < n_mp:
                alpha.append(swap(sums.pop(bit), bit, n_mp))
                for b in [b for b in sums if b & bit]:
                    sums[b ^ bit] = add_low(sums[b ^ bit], swap(sums.pop(b), bit, n_mp))
                bit *= 2
            for reduction in (grad_down, grad_gate, grad_up):
                reduction.step()
        if i == pairs[-1]:
            far_pairs = [order.tie(g)[rest] for g in g_pairs]
            total = sum(dot_nt(g, w) for g, w in zip(far_pairs, w_pairs))
            far_terms, sent = scatter_far(cut(total.astype(BF)), n_mp, order)
            order.mark(sent)
            alpha = sum(t.astype(F32) for t in order.tie(*alpha))
            small = [jnp.concatenate(s_pairs)[:, 0], unit_scales[0], unit_scales[1], *alpha]
            lengths = [t.shape[0] // n_dp for t in small]
            extra = jnp.concatenate([t.reshape(n_dp, 1, -1) for t in small], axis=2).astype(BF)
            columns = 3 * PAIR + (width if i == 0 else 0)
            extra = jnp.pad(extra, ((0, 0), (0, 15), (0, columns - extra.shape[2])))
        grads = [rows_first(dot_tn(order.tie(x_all), g_pair))]
        if i == 0:
            grad_out = lax.dot_general(a_all, order.tie(o), (((0,), (1,)), ((), ())), preferred_element_type=F32)
            grads.append(rows_first(grad_out))
        grads = jnp.concatenate(grads, axis=1)
        if i == pairs[-1]:
            grads = jnp.concatenate([grads.reshape(n_dp, -1, columns), extra], axis=1).reshape(-1, columns)
        joints.append(Reduction(order, grads, x_first, place))
        order.mark(grads)

    def finish(reduction):
        while reduction.bits:
            reduction.step()
        return reduction.step()

    order.mark(sent)
    joints[0].step()
    bulk = []
    for reduction in (grad_gate, grad_up, grad_down):
        order.mark(sent)
        bulk.append(finish(reduction))
    grad_gate, grad_up, grad_down = bulk
    order.mark(sent)
    near_pairs = [order.tie(g)[near] for g in g_pairs]
    total = sum(dot_nt(g, w) for g, w in zip(near_pairs, w_pairs))
    parts = cut(order.mark(total.astype(BF)))
    in_terms = [parts[0], swap(parts[1], 1, n_mp), *far_terms]
    for reduction in joints[::-1]:
        reduction.step()
    in_terms[-1] = order.fill(sent, order.tie(in_terms[-1]))
    grad_input = input_update(in_terms, grad_x, order.hint)
    order.mark(grad_input)
    joints[-1].step()
    joints = [finish(reduction) for reduction in joints]
    ends = [sum(lengths[: i + 1]) for i in range(len(lengths))]
    extra, joints[-1] = joints[-1][-16], joints[-1][:-16]
    score, up_share, gate_share, alpha_a, alpha_f = [extra[e - n : e] for e, n in zip(ends, lengths)]
    grad_query, grad_key, grad_value = [
        jnp.concatenate([joint[:, i * PAIR : (i + 1) * PAIR] for joint in joints], axis=1) for i in range(3)
    ]
    grad_out, grad_down = joints[0][: depth // n_dp, 3 * PAIR :].T, grad_down.T
    return (
        layer_out,
        grad_input,
        grad_query,
        grad_key,
        grad_value,
        grad_out,
        grad_up,
        grad_gate,
        grad_down,
        score,
        up_share,
        gate_share,
        alpha_a,
        alpha_f,
    )


def solution(mesh):
    n_dp, n_mp = mesh.shape["dp"], mesh.shape["mp"]
    bits = [1 << i for i in range(n_dp.bit_length() - 1)]
    cut = len(bits) // 2
    token = P(("dp", "mp"), None)
    split = P(("mp", "dp"))
    return jax.shard_map(
        partial(body, n_mp, bits[:cut], bits[cut:]),
        mesh=mesh,
        in_specs=(
            token, P("dp"), P("dp"), P(None, "mp"), P(None, "mp"), P(None, "mp"), P("mp", None),
            P(None, "mp"), P(None, "mp"), P("mp", None), P("mp"), P("mp"), P("mp"), P(), P(), token,
        ),
        out_specs=(
            token, token, P("dp", "mp"), P("dp", "mp"), P("dp", "mp"), P("mp", "dp"),
            P("dp", "mp"), P("dp", "mp"), P("mp", "dp"), split, split, split, split, split,
        ),
        check_vma=False,
    )
```

time: 721 us -> 281 us (0.39)
  waiting for transfers between devices: 389 us -> 82.7 us
  matrix products: 182 us -> 43.8 us
  Pallas kernels: 0 us -> 53.5 us
  starting transfers between devices: 1.21 us -> 30.1 us
  blocking collectives: 21.6 us -> 0 us
  local copies, waits for them, and re-layouts: 49.2 us -> 28.1 us
  between operations: 16.5 us -> 1.84 us
  other arithmetic: 45 us -> 36 us
  loops' own time: 8.5 us -> 0 us
    reduce_scatter x5 -> x0, waiting for transfers between devices: 213 us -> none  [the longest x1 89.4 us: body(): lax.psum_scatter(grad_w_pair.astype(jnp.bfloat16), 'dp', scatter_dimensio...]
    dot_general x26, matrix products: 182 us -> 43.8 us  [the longest x12 18.1 us: dot_nt(): lax.dot_general(left, right, (((1,), (1,)), ((), ())), preferred_element_...]
    unnamed x19 -> x0, waiting for transfers between devices: 92.4 us -> none
    all_gather x4 -> x0, waiting for transfers between devices: 82.9 us -> none  [the longest x1 24.7 us: body(): grad_rows_all = lax.all_gather(grad_mixed_low, 'mp', axis=0, tiled=True)]
    ppermute x0 -> x42, waiting for transfers between devices: none -> 82.7 us  [swap(): return lax.ppermute(value, name, [(i, i ^ bit) for i in range(size)])]
    pallas_call x0 -> x15, Pallas kernels: none -> 53.5 us  [the longest x2 15.7 us: attend_back(): pl.pallas_call(attend_back_kernel, grid_spec=pltpu.PrefetchScalarGridSpec...]
    ppermute x0 -> x42, starting transfers between devices: none -> 30.1 us  [swap(): return lax.ppermute(value, name, [(i, i ^ bit) for i in range(size)])]
    unnamed x1 -> x0, blocking collectives: 21.6 us -> none
  transfers between devices with their start and end apart: 14 -> 42, of which waited for: 12 -> 22; matrix products, arithmetic and copies ran while one was open for 25% -> 30% of each run, Pallas kernels for 0% -> 13%
where the time goes in v1:
time: 281 us; the launch traced here: 276 us
  waiting for transfers between devices  82.7 us (29%)
  Pallas kernels  53.5 us (19%)
  matrix products  43.8 us (16%)
  other arithmetic  36 us (13%)
  starting transfers between devices  30.1 us (11%)
  local copies, waits for them, and re-layouts  28.1 us (10%)
    ppermute x42, waiting for transfers between devices, swap(): return lax.ppermute(value, name, [(i, i ^ bit) for i in range(size)])  82.7 us
    ppermute x42, starting transfers between devices, swap(): return lax.ppermute(value, name, [(i, i ^ bit) for i in range(size)])  30.1 us
    convert_element_type x15, other arithmetic, add_low(): return (left.astype(F32) + right.astype(F32)).astype(BF)  19.1 us
    dot_general x12, matrix products, dot_nt(): lax.dot_general(left, right, (((1,), (1,)), ((), ())), preferred_element_...  18.1 us
    pallas_call x2, Pallas kernels, attend_back(): pl.pallas_call(attend_back_kernel, grid_spec=pltpu.PrefetchScalarGridSpec...  15.7 us
    pallas_call x4, Pallas kernels, row_call(): pl.pallas_call(kernel, grid=(1,), in_specs=[whole_spec((BLOCK, depth))] *...  15.2 us
    dot_general x7, matrix products, dot_tn(): lax.dot_general(left, right, (((0,), (0,)), ((), ())), preferred_element_...  13.3 us
    unnamed x161, local copies, waits for them, and re-layouts  11.8 us
  transfers between devices with their start and end apart: 42, of which 22 were waited for; matrix products, arithmetic and copies ran while one was open for 30% of the time, Pallas kernels for 13%

profile of v1, /device:TPU:0, one launch (start us, length us, event | category | flops | bytes accessed | tf_op | source)
XLA Modules:
  0.0 276.1 jit_solution(10383776919069707996)
XLA Ops:
  0.7 3.0 %collective-permute-start = (bf16[256,1024]{1,0:T(8,128)(2,1)}, bf16[256,1024]{1,0:T(8,128)(2,1)S(1)}, u32[]{:S(2)}, u32[]{:S(2)}) collective-permute-start(bf16[256,1024]{1,0:T(8,128)(2,1)} %refs_6_.1), channel_id=1, source_target_pairs={{0,2},{1,3},{2,0},{3,1},{4,6},{5,7},{6,4},{7,5},{8,10},{9,11},{10,... | collective-permute-start | bytes 1572872 | tf_op jit(solution)/shard_map/ppermute | solution.py:22
  3.7 1.5 copy.75.refs_7_.scale_ref
  5.2 1.4 iota_subtract_fusion
  8.6 3.7 %project.2 = (bf16[256,1024]{1,0:T(8,128)(2,1)}, bf16[256,1024]{1,0:T(8,128)(2,1)}, bf16[256,1024]{1,0:T(8,128)(2,1)}, f32[4,1,1024]{2,1,0:T(1,128)}, f32[4,1,1024]{2,1,0:T(1,128)}) custom-call(s32[1]{0:T(128)} %bitcast.me_ref, bf16[256,1024]{1,0:T(8,128)(2,1)} %refs_6_.1, bf16[256,1024]{1,0:T(8,128)(2,1)} %copy-done.23, bf16[1024,256]{1,0:T(8,128)(2,1)} %refs_2_.3, ...), custom_call_target="tpu_custom_call" | custom-call | flops 1 | bytes 1 | tf_op jit(solution)/shard_map/project/pallas_call | solution.py:199
  12.3 3.6 %collective-permute-done.refs_0_ = bf16[256,1024]{1,0:T(8,128)(2,1)S(1)} collective-permute-done((bf16[256,1024]{1,0:T(8,128)(2,1)}, bf16[256,1024]{1,0:T(8,128)(2,1)S(1)}, u32[]{:S(2)}, u32[]{:S(2)}) %collective-permute-start) | collective-permute-done | bytes 524320 | tf_op jit(solution)/shard_map/ppermute | solution.py:22
  15.8 1.9 collective-permute-done.2.refs_1_
  18.5 3.7 %project.3 = (bf16[256,1024]{1,0:T(8,128)(2,1)}, bf16[256,1024]{1,0:T(8,128)(2,1)}, bf16[256,1024]{1,0:T(8,128)(2,1)}, f32[4,1,1024]{2,1,0:T(1,128)}, f32[4,1,1024]{2,1,0:T(1,128)}) custom-call(s32[1]{0:T(128)} %bitcast.me_ref, bf16[256,1024]{1,0:T(8,128)(2,1)} %copy-done.21, ...), custom_call_target="tpu_custom_call", output_to_operand_aliasing={{0}: (9, {}), {1}: (10, {}), {2}: (11, {}), {3}: (12, {}), ... | custom-call | flops 1 | bytes 1 | tf_op jit(solution)/shard_map/project/pallas_call | solution.py:199
  22.3 7.2 %attend.1 = (bf16[256,1024]{1,0:T(8,128)(2,1)}, f32[4,1,1024]{2,1,0:T(1,128)}) custom-call(s32[1]{0:T(128)} %bitcast.me_ref, bf16[256,1024]{1,0:T(8,128)(2,1)} %get-tuple-element.120.q_ref, bf16[256,1024]{1,0:T(8,128)(2,1)} %get-tuple-element.121.k_ref, bf16[256,1024]{1,0:T(8,128)(2,1)} %get-tuple-element.122.v_ref, s32[1,1024]{1,0:T(1,128)} %bitcast.170), custom_call_target="tpu_custom_call" | custom-call | flops 2147483648 | bytes 2097152 | tf_op jit(solution)/shard_map/attend/pallas_call | solution.py:258
  29.5 1.5 convolution_convert_fusion.4
  31.3 1.8 collective-permute-done.3
  34.8 1.8 collective-permute-start.5
  36.5 12.4 %collective-permute-done.5.refs_2_ = bf16[256,1024]{1,0:T(8,128)(2,1)S(1)} collective-permute-done((bf16[256,1024]{1,0:T(8,128)(2,1)S(1)}, bf16[256,1024]{1,0:T(8,128)(2,1)S(1)}, u32[]{:S(2)}, u32[]{:S(2)}) %collective-permute-start.5) | collective-permute-done | bytes 524320 | tf_op jit(solution)/shard_map/ppermute | solution.py:22
  49.8 3.4 %middle_update.1 = (f32[256,1024]{1,0:T(8,128)}, bf16[256,1024]{1,0:T(8,128)(2,1)}) custom-call(bf16[256,1024]{1,0:T(8,128)(2,1)} %get-tuple-element.312.refs_0_, bf16[256,1024]{1,0:T(8,128)(2,1)} %copy-done.31, bf16[256,1024]{1,0:T(8,128)(2,1)} %copy-done.32, bf16[256,1024]{1,0:T(8,128)(2,1)} %refs_6_.1, f32[1,1024]{1,0:T(1,128)} %bitcast.174), custom_call_target="tpu_custom_call" | custom-call | flops 1 | bytes 1 | tf_op jit(solution)/shard_map/middle_update/pallas_call | solution.py:388
  53.2 1.7 collective-permute-start.7
  58.5 2.6 multiply_convert_fusion.5
  62.4 5.3 %collective-permute-done.7 = bf16[256,1024]{1,0:T(8,128)(2,1)S(1)} collective-permute-done((bf16[256,1024]{1,0:T(8,128)(2,1)}, bf16[256,1024]{1,0:T(8,128)(2,1)S(1)}, u32[]{:S(2)}, u32[]{:S(2)}) %collective-permute-start.7) | collective-permute-done | bytes 524320 | tf_op jit(solution)/shard_map/ppermute | solution.py:22
  67.8 1.9 collective-permute-done.8
  71.0 2.6 multiply_convert_fusion.4
  75.1 1.8 collective-permute-done.9
  79.1 1.8 collective-permute-start.11
  82.0 11.6 %collective-permute-done.11.refs_2_ = bf16[256,1024]{1,0:T(8,128)(2,1)} collective-permute-done((bf16[256,1024]{1,0:T(8,128)(2,1)}, bf16[256,1024]{1,0:T(8,128)(2,1)}, u32[]{:S(2)}, u32[]{:S(2)}) %collective-permute-start.11) | collective-permute-done | bytes 524320 | tf_op jit(solution)/shard_map/ppermute | solution.py:22
  93.6 4.2 %last_update.1 = (bf16[256,1024]{1,0:T(8,128)(2,1)}, f32[256,1024]{1,0:T(8,128)}, bf16[256,1024]{1,0:T(8,128)(2,1)}, f32[1,1024]{1,0:T(1,128)}) custom-call(bf16[256,1024]{1,0:T(8,128)(2,1)} %get-tuple-element.310.refs_0_, bf16[256,1024]{1,0:T(8,128)(2,1)} %collective-permute-done.10.refs_1_, bf16[256,1024]{1,0:T(8,128)(2,1)} %collective-permute-done.11.refs_2_, ...), custom_call_target="tpu_custom_call" | custom-call | flops 1 | bytes 1 | tf_op jit(solution)/shard_map/last_update/pallas_call | solution.py:388
  98.6 1.5 pad_maximum_fusion.2
  101.9 1.7 collective-permute-start.13
  103.7 2.4 multiply_convert_fusion.2
  108.4 2.3 add_convert_fusion.3
  110.7 5.5 %collective-permute-done.13 = bf16[256,1024]{1,0:T(8,128)(2,1)S(1)} collective-permute-done((bf16[256,1024]{1,0:T(8,128)(2,1)S(1)}, bf16[256,1024]{1,0:T(8,128)(2,1)S(1)}, u32[]{:S(2)}, u32[]{:S(2)}) %collective-permute-start.13) | collective-permute-done | bytes 524320 | tf_op jit(solution)/shard_map/ppermute | solution.py:22
  116.3 1.5 pad_maximum_fusion
  118.2 2.4 convolution_convert_fusion
  121.8 1.7 collective-permute-start.20
  123.5 3.3 %fusion.25 = (f32[1024]{0:T(1024)S(1)}, f32[1024]{0:T(1024)S(1)}, f32[1024]{0:T(1024)S(1)}, f32[1024]{0:T(1024)S(1)}, f32[512,1024]{1,0:T(8,128)S(1)}, /*index=5*/bf16[512,1024]{1,0:T(8,128)(2,1)S(1)}) fusion(f32[512,1024]{1,0:T(8,128)S(1)} %copy-done.69, f32[1024]{0:T(1024)S(1)} %copy-done.56, bf16[512,1024]{1,0:T(8,128)(2,1)S(1)} %copy-done.76, ...), kind=kOutput, calls=%fused_computation.33 | convolution fusion | flops 1092087808 | bytes 16801792 | tf_op jit(solution)/shard_map/dot_general | solution.py:155
  128.4 1.5 add_convert_fusion.2
  131.7 1.4 stand_in.6.mark_ref
  133.2 2.2 add_convert_fusion.11.sent_ref
  135.4 1.5 collective-permute-start.17
  136.9 3.9 %fusion.45 = bf16[1024,1024]{1,0:T(8,128)(2,1)S(1)} fusion(bf16[1024,1024]{1,0:T(8,128)(2,1)S(1)} %copy-done.19, bf16[512,1024]{1,0:T(8,128)(2,1)} %copy-done.35, bf16[512,1024]{1,0:T(8,128)(2,1)} %copy-done.70), kind=kOutput, calls=%fused_computation.64 | convolution fusion | flops 2152726528 | bytes 6291456 | tf_op jit(solution)/shard_map/dot_general | solution.py:151
  143.4 2.5 fusion.42
  148.2 1.6 collective-permute-start.23
  153.0 4.6 %middle_back.1 = (f32[256,1024]{1,0:T(8,128)}, bf16[256,1024]{1,0:T(8,128)(2,1)}, f32[1,1024]{1,0:T(1,128)}) custom-call(bf16[256,1024]{1,0:T(8,128)(2,1)} %get-tuple-element.312.refs_0_, bf16[256,1024]{1,0:T(8,128)(2,1)} %copy-done.31, bf16[256,1024]{1,0:T(8,128)(2,1)} %copy-done.32, bf16[256,1024]{1,0:T(8,128)(2,1)} %get-tuple-element.308.refs_3_, ...), custom_call_target="tpu_custom_call" | custom-call | flops 1 | bytes 1 | tf_op jit(solution)/shard_map/middle_back/pallas_call | solution.py:388
  159.5 12.4 %collective-permute-done.19.sent_ref = bf16[256,1024]{1,0:T(8,128)(2,1)} collective-permute-done((bf16[256,1024]{1,0:T(8,128)(2,1)}, bf16[256,1024]{1,0:T(8,128)(2,1)}, u32[]{:S(2)}, u32[]{:S(2)}) %collective-permute-start.19) | collective-permute-done | bytes 524320 | tf_op jit(solution)/shard_map/ppermute | solution.py:22
  174.9 2.6 add_convert_fusion.5
  177.5 1.3 stand_in.9.mark_ref
  180.2 1.7 fusion.52
  182.8 2.4 add_convert_fusion.6
  186.2 2.4 add_convert_fusion.7
  188.6 1.6 collective-permute-start.24
  190.2 8.0 %attend_back.2 = (bf16[1024,384]{1,0:T(8,128)(2,1)}, f32[128,1]{1,0:T(8,128)}) custom-call(s32[1]{0:T(128)} %bitcast.me_ref, bf16[256,1024]{1,0:T(8,128)(2,1)} %get-tuple-element.120.q_ref, bf16[256,1024]{1,0:T(8,128)(2,1)} %get-tuple-element.121.k_ref, bf16[256,1024]{1,0:T(8,128)(2,1)} %get-tuple-element.122.v_ref, ...), custom_call_target="tpu_custom_call" | custom-call | flops 1 | bytes 1 | tf_op jit(solution)/shard_map/attend_back/pallas_call | solution.py:357
  200.8 2.6 collective-permute-start.41
  203.4 2.0 fusion.74
  205.5 3.5 %collective-permute-done.24 = bf16[256,1024]{1,0:T(8,128)(2,1)S(1)} collective-permute-done((bf16[256,1024]{1,0:T(8,128)(2,1)}, bf16[256,1024]{1,0:T(8,128)(2,1)S(1)}, u32[]{:S(2)}, u32[]{:S(2)}) %collective-permute-start.24) | collective-permute-done | bytes 524320 | tf_op jit(solution)/shard_map/ppermute | solution.py:22
  211.3 2.1 fusion.48
  213.6 7.7 %attend_back.3 = (bf16[1024,384]{1,0:T(8,128)(2,1)}, f32[128,1]{1,0:T(8,128)}) custom-call(s32[1]{0:T(128)} %bitcast.me_ref, bf16[256,1024]{1,0:T(8,128)(2,1)} %get-tuple-element.120.q_ref, bf16[256,1024]{1,0:T(8,128)(2,1)} %get-tuple-element.121.k_ref, bf16[256,1024]{1,0:T(8,128)(2,1)} %get-tuple-element.122.v_ref, ...), custom_call_target="tpu_custom_call" | custom-call | flops 1 | bytes 1 | tf_op jit(solution)/shard_map/attend_back/pallas_call | solution.py:357
  221.4 2.9 %collective-permute-start.40 = (bf16[128,1024]{1,0:T(8,128)(2,1)}, bf16[128,1024]{1,0:T(8,128)(2,1)}, u32[]{:S(2)}, u32[]{:S(2)}) collective-permute-start(bf16[128,1024]{1,0:T(8,128)(2,1)} %get-tuple-element.302), channel_id=1, source_target_pairs={{0,16},{4,20},{8,24},{12,28},{16,0},{20,4},{24,8},{28,12},{1,17},{... | collective-permute-start | bytes 786440 | tf_op jit(solution)/shard_map/ppermute | solution.py:22
  226.9 1.3 stand_in.10.mark_ref
  230.4 2.0 add_convert_fusion.4.sent_ref
  238.1 1.8 collective-permute-done.39
  240.8 1.8 convert_add_fusion.1
  242.6 2.8 %collective-permute-done.40 = bf16[128,1024]{1,0:T(8,128)(2,1)} collective-permute-done((bf16[128,1024]{1,0:T(8,128)(2,1)}, bf16[128,1024]{1,0:T(8,128)(2,1)}, u32[]{:S(2)}, u32[]{:S(2)}) %collective-permute-start.40) | collective-permute-done | bytes 262176 | tf_op jit(solution)/shard_map/ppermute | solution.py:22
  245.5 1.8 collective-permute-done.30
  248.6 1.8 convert_add_fusion
  250.4 5.8 %collective-permute-done.35 = bf16[576,384]{1,0:T(8,128)(2,1)S(1)} collective-permute-done((bf16[576,384]{1,0:T(8,128)(2,1)S(1)}, bf16[576,384]{1,0:T(8,128)(2,1)S(1)}, u32[]{:S(2)}, u32[]{:S(2)}) %collective-permute-start.35) | collective-permute-done | bytes 442400 | tf_op jit(solution)/shard_map/ppermute | solution.py:22
  261.1 3.0 %input_update.1 = f32[256,1024]{1,0:T(8,128)} custom-call(bf16[256,1024]{1,0:T(8,128)(2,1)} %get-tuple-element.306.refs_0_, bf16[256,1024]{1,0:T(8,128)(2,1)} %copy-done.47, bf16[256,1024]{1,0:T(8,128)(2,1)} %collective-permute-done.29.refs_2_, f32[256,1024]{1,0:T(8,128)} %get-tuple-element.200.refs_3_, f32[8,128]{1,0:T(8,128)} %stand_in.11.refs_4_), custom_call_target="tpu_custom_call" | custom-call | flops 1 | bytes 1 | tf_op jit(solution)/shard_map/input_update/pallas_call | solution.py:388
  264.1 1.7 collective-permute-done.37
  269.5 3.2 %collective-permute-done.38 = bf16[144,384]{1,0:T(8,128)(2,1)S(1)} collective-permute-done((bf16[144,384]{1,0:T(8,128)(2,1)S(1)}, bf16[144,384]{1,0:T(8,128)(2,1)S(1)}, u32[]{:S(2)}, u32[]{:S(2)}) %collective-permute-start.38) | collective-permute-done | bytes 110624 | tf_op jit(solution)/shard_map/ppermute | solution.py:22
  (296 shorter events, 71.9 us)
Async XLA Ops:
  0.6 60.5 %copy-start = (bf16[1024,1024]{1,0:T(8,128)(2,1)S(1)}, bf16[1024,1024]{1,0:T(8,128)(2,1)}, u32[]{:S(2)}) copy-start(bf16[1024,1024]{1,0:T(8,128)(2,1)} %param.24) | copy-start | bytes 6291460
  0.7 15.2 %collective-permute-start = (bf16[256,1024]{1,0:T(8,128)(2,1)}, bf16[256,1024]{1,0:T(8,128)(2,1)S(1)}, u32[]{:S(2)}, u32[]{:S(2)}) collective-permute-start(bf16[256,1024]{1,0:T(8,128)(2,1)} %refs_6_.1), channel_id=1, source_target_pairs={{0,2},{1,3},{2,0},{3,1},{4,6},{5,7},{6,4},{7,5},{8,10},{9,11},{10,... | collective-permute-start | bytes 1572872 | tf_op jit(solution)/shard_map/ppermute | solution.py:22
  3.7 4.1 %collective-permute-start.1 = (bf16[256,1024]{1,0:T(8,128)(2,1)}, bf16[256,1024]{1,0:T(8,128)(2,1)S(1)}, u32[]{:S(2)}, u32[]{:S(2)}) collective-permute-start(bf16[256,1024]{1,0:T(8,128)(2,1)} %refs_6_.1), channel_id=1, source_target_pairs={{0,1},{1,0},{2,3},{3,2},{4,5},{5,4},{6,7},{7,6},{8,9},{9,8},{10,11... | collective-permute-start | bytes 1572872 | tf_op jit(solution)/shard_map/ppermute | solution.py:22
  15.8 1.9 collective-permute-start.2
  22.3 7.2 %copy-start.14 = (bf16[256,1024]{1,0:T(8,128)(2,1)S(1)}, bf16[256,1024]{1,0:T(8,128)(2,1)}, u32[]{:S(2)}) copy-start(bf16[256,1024]{1,0:T(8,128)(2,1)} %param.21) | copy-start | bytes 1572868
  31.1 2.0 collective-permute-start.3
  34.6 1.9 collective-permute-start.4
  34.8 14.2 %collective-permute-start.5 = (bf16[256,1024]{1,0:T(8,128)(2,1)S(1)}, bf16[256,1024]{1,0:T(8,128)(2,1)S(1)}, u32[]{:S(2)}, u32[]{:S(2)}) collective-permute-start(bf16[256,1024]{1,0:T(8,128)(2,1)S(1)} %add_convert_fusion.13), channel_id=1, source_target_pairs={{0,2},{1,3},{2,0},{3,1},{4,6},{5,7},{6,4},{7,5},{8,10},{9,11},{10,... | collective-permute-start | bytes 1572872 | tf_op jit(solution)/shard_map/ppermute | solution.py:22
  36.5 12.4 %copy-start.31 = (bf16[256,1024]{1,0:T(8,128)(2,1)}, bf16[256,1024]{1,0:T(8,128)(2,1)S(1)}, u32[]{:S(2)}) copy-start(bf16[256,1024]{1,0:T(8,128)(2,1)S(1)} %collective-permute-done.4.refs_1_) | copy-start | bytes 1572868
  49.8 7.1 %copy-start.59 = (bf16[1024,1024]{1,0:T(8,128)(2,1)S(1)}, bf16[1024,1024]{1,0:T(8,128)(2,1)}, u32[]{:S(2)}) copy-start(bf16[1024,1024]{1,0:T(8,128)(2,1)} %param.22) | copy-start | bytes 6291460
  53.2 2.9 %collective-permute-start.6 = (bf16[256,1024]{1,0:T(8,128)(2,1)}, bf16[256,1024]{1,0:T(8,128)(2,1)S(1)}, u32[]{:S(2)}, u32[]{:S(2)}) collective-permute-start(bf16[256,1024]{1,0:T(8,128)(2,1)} %get-tuple-element.125), channel_id=1, source_target_pairs={{0,1},{1,0},{2,3},{3,2},{4,5},{5,4},{6,7},{7,6},{8,9},{9,8},{10,11... | collective-permute-start | bytes 1572872 | tf_op jit(solution)/shard_map/ppermute | solution.py:22
  53.2 14.5 %collective-permute-start.7 = (bf16[256,1024]{1,0:T(8,128)(2,1)}, bf16[256,1024]{1,0:T(8,128)(2,1)S(1)}, u32[]{:S(2)}, u32[]{:S(2)}) collective-permute-start(bf16[256,1024]{1,0:T(8,128)(2,1)} %get-tuple-element.125), channel_id=1, source_target_pairs={{0,2},{1,3},{2,0},{3,1},{4,6},{5,7},{6,4},{7,5},{8,10},{9,11},{10,... | collective-permute-start | bytes 1572872 | tf_op jit(solution)/shard_map/ppermute | solution.py:22
  67.7 1.9 collective-permute-start.8
  74.9 5.9 %copy-start.6 = (bf16[1024,256]{1,0:T(8,128)(2,1)S(1)}, bf16[1024,256]{1,0:T(8,128)(2,1)}, u32[]{:S(2)}) copy-start(bf16[1024,256]{1,0:T(8,128)(2,1)} %refs_2_.3) | copy-start | bytes 1572868
  74.9 5.9 %copy-start.7 = (bf16[1024,256]{1,0:T(8,128)(2,1)S(1)}, bf16[1024,256]{1,0:T(8,128)(2,1)}, u32[]{:S(2)}) copy-start(bf16[1024,256]{1,0:T(8,128)(2,1)} %refs_3_.4) | copy-start | bytes 1572868
  74.9 2.0 collective-permute-start.9
  79.0 3.0 %collective-permute-start.10 = (bf16[256,1024]{1,0:T(8,128)(2,1)}, bf16[256,1024]{1,0:T(8,128)(2,1)}, u32[]{:S(2)}, u32[]{:S(2)}) collective-permute-start(bf16[256,1024]{1,0:T(8,128)(2,1)} %get-tuple-element.309), channel_id=1, source_target_pairs={{0,1},{1,0},{2,3},{3,2},{4,5},{5,4},{6,7},{7,6},{8,9},{9,8},{10,11... | collective-permute-start | bytes 1572872 | tf_op jit(solution)/shard_map/ppermute | solution.py:22
  79.1 14.5 %collective-permute-start.11 = (bf16[256,1024]{1,0:T(8,128)(2,1)}, bf16[256,1024]{1,0:T(8,128)(2,1)}, u32[]{:S(2)}, u32[]{:S(2)}) collective-permute-start(bf16[256,1024]{1,0:T(8,128)(2,1)} %add_convert_fusion.12), channel_id=1, source_target_pairs={{0,2},{1,3},{2,0},{3,1},{4,6},{5,7},{6,4},{7,5},{8,10},{9,11},{10,... | collective-permute-start | bytes 1572872 | tf_op jit(solution)/shard_map/ppermute | solution.py:22
  82.0 15.8 %copy-start.5 = (bf16[1024,256]{1,0:T(8,128)(2,1)S(1)}, bf16[1024,256]{1,0:T(8,128)(2,1)}, u32[]{:S(2)}) copy-start(bf16[1024,256]{1,0:T(8,128)(2,1)} %refs_4_.4) | copy-start | bytes 1572868
  93.6 4.9 %copy-start.26 = (bf16[256,1024]{1,0:T(8,128)(2,1)S(1)}, bf16[256,1024]{1,0:T(8,128)(2,1)}, u32[]{:S(2)}) copy-start(bf16[256,1024]{1,0:T(8,128)(2,1)} %copy-done.25) | copy-start | bytes 1572868
  97.8 5.8 %collective-permute-start.12 = (bf16[256,1024]{1,0:T(8,128)(2,1)}, bf16[256,1024]{1,0:T(8,128)(2,1)S(1)}, u32[]{:S(2)}, u32[]{:S(2)}) collective-permute-start(bf16[256,1024]{1,0:T(8,128)(2,1)} %get-tuple-element.130), channel_id=1, source_target_pairs={{0,1},{1,0},{2,3},{3,2},{4,5},{5,4},{6,7},{7,6},{8,9},{9,8},{10,11... | collective-permute-start | bytes 1572872 | tf_op jit(solution)/shard_map/ppermute | solution.py:22
  101.9 14.3 %collective-permute-start.13 = (bf16[256,1024]{1,0:T(8,128)(2,1)S(1)}, bf16[256,1024]{1,0:T(8,128)(2,1)S(1)}, u32[]{:S(2)}, u32[]{:S(2)}) collective-permute-start(bf16[256,1024]{1,0:T(8,128)(2,1)S(1)} %copy-done.45), channel_id=1, source_target_pairs={{0,2},{1,3},{2,0},{3,1},{4,6},{5,7},{6,4},{7,5},{8,10},{9,11},{10,... | collective-permute-start | bytes 1572872 | tf_op jit(solution)/shard_map/ppermute | solution.py:22
  108.4 7.8 %copy-start.13 = (bf16[512,1024]{1,0:T(8,128)(2,1)S(1)}, bf16[512,1024]{1,0:T(8,128)(2,1)}, u32[]{:S(2)}) copy-start(bf16[512,1024]{1,0:T(8,128)(2,1)} %copy-done.12) | copy-start | bytes 3145732
  108.4 7.8 %copy-start.28 = (bf16[256,1024]{1,0:T(8,128)(2,1)S(1)}, bf16[256,1024]{1,0:T(8,128)(2,1)}, u32[]{:S(2)}) copy-start(bf16[256,1024]{1,0:T(8,128)(2,1)} %get-tuple-element.125) | copy-start | bytes 1572868
  108.4 7.8 %copy-start.30 = (bf16[256,1024]{1,0:T(8,128)(2,1)S(1)}, bf16[256,1024]{1,0:T(8,128)(2,1)}, u32[]{:S(2)}) copy-start(bf16[256,1024]{1,0:T(8,128)(2,1)} %copy-done.29) | copy-start | bytes 1572868
  116.2 1.9 collective-permute-start.14
  121.8 53.1 %collective-permute-start.20 = (bf16[512,1024]{1,0:T(8,128)(2,1)}, bf16[512,1024]{1,0:T(8,128)(2,1)}, u32[]{:S(2)}, u32[]{:S(2)}) collective-permute-start(bf16[512,1024]{1,0:T(8,128)(2,1)} %bitcast.6), channel_id=1, source_target_pairs={{0,4},{4,0},{8,12},{12,8},{16,20},{20,16},{24,28},{28,24},{1,5},{5... | collective-permute-start | bytes 3145736 | tf_op jit(solution)/shard_map/ppermute | solution.py:22
  130.9 2.3 collective-permute-start.15
  131.7 5.2 %copy-start.19 = (bf16[1024,1024]{1,0:T(8,128)(2,1)S(1)}, bf16[1024,1024]{1,0:T(8,128)(2,1)}, u32[]{:S(2)}) copy-start(bf16[1024,1024]{1,0:T(8,128)(2,1)} %pad_maximum_fusion) | copy-start | bytes 6291460
  135.4 16.7 %collective-permute-start.17 = (bf16[256,1024]{1,0:T(8,128)(2,1)}, bf16[256,1024]{1,0:T(8,128)(2,1)}, u32[]{:S(2)}, u32[]{:S(2)}) collective-permute-start(bf16[256,1024]{1,0:T(8,128)(2,1)} %add_convert_fusion.11.sent_ref), channel_id=1, source_target_pairs={{0,2},{1,3},{2,0},{3,1},{4,6},{5,7},{6,4},{7,5},{8,10},{9,11},{10,... | collective-permute-start | bytes 1572872 | tf_op jit(solution)/shard_map/ppermute | solution.py:22
  147.1 39.1 %collective-permute-start.22 = (bf16[512,1024]{1,0:T(8,128)(2,1)}, bf16[512,1024]{1,0:T(8,128)(2,1)}, u32[]{:S(2)}, u32[]{:S(2)}) collective-permute-start(bf16[512,1024]{1,0:T(8,128)(2,1)} %bitcast.10), channel_id=1, source_target_pairs={{0,4},{4,0},{8,12},{12,8},{16,20},{20,16},{24,28},{28,24},{1,5},{5... | collective-permute-start | bytes 3145736 | tf_op jit(solution)/shard_map/ppermute | solution.py:22
  148.2 34.6 %collective-permute-start.23 = (bf16[512,1024]{1,0:T(8,128)(2,1)}, bf16[512,1024]{1,0:T(8,128)(2,1)}, u32[]{:S(2)}, u32[]{:S(2)}) collective-permute-start(bf16[512,1024]{1,0:T(8,128)(2,1)} %bitcast.8), channel_id=1, source_target_pairs={{0,8},{4,12},{8,0},{12,4},{16,24},{20,28},{24,16},{28,20},{1,9},{5... | collective-permute-start | bytes 3145736 | tf_op jit(solution)/shard_map/ppermute | solution.py:22
  150.8 2.3 collective-permute-start.16
  157.7 14.3 %collective-permute-start.19 = (bf16[256,1024]{1,0:T(8,128)(2,1)}, bf16[256,1024]{1,0:T(8,128)(2,1)}, u32[]{:S(2)}, u32[]{:S(2)}) collective-permute-start(bf16[256,1024]{1,0:T(8,128)(2,1)} %get-tuple-element.144.sent_ref), channel_id=1, source_target_pairs={{0,2},{1,3},{2,0},{3,1},{4,6},{5,7},{6,4},{7,5},{8,10},{9,11},{10,... | collective-permute-start | bytes 1572872 | tf_op jit(solution)/shard_map/ppermute | solution.py:22
  158.2 13.8 %collective-permute-start.18 = (bf16[256,1024]{1,0:T(8,128)(2,1)}, bf16[256,1024]{1,0:T(8,128)(2,1)}, u32[]{:S(2)}, u32[]{:S(2)}) collective-permute-start(bf16[256,1024]{1,0:T(8,128)(2,1)} %get-tuple-element.144.sent_ref), channel_id=1, source_target_pairs={{0,1},{1,0},{2,3},{3,2},{4,5},{5,4},{6,7},{7,6},{8,9},{9,8},{10,11... | collective-permute-start | bytes 1572872 | tf_op jit(solution)/shard_map/ppermute | solution.py:22
  159.5 14.3 %copy-start.15 = (bf16[256,1024]{1,0:T(8,128)(2,1)S(1)}, bf16[256,1024]{1,0:T(8,128)(2,1)}, u32[]{:S(2)}) copy-start(bf16[256,1024]{1,0:T(8,128)(2,1)} %param.21) | copy-start | bytes 1572868
  172.0 27.2 %collective-permute-start.32 = (bf16[2,256]{1,0:T(2,128)(2,1)S(1)}, bf16[2,256]{1,0:T(2,128)(2,1)S(1)}, u32[]{:S(2)}, u32[]{:S(2)}) collective-permute-start(bf16[2,256]{1,0:T(2,128)(2,1)S(1)} %get-tuple-element.342), channel_id=1, source_target_pairs={{0,1},{1,0},{2,3},{3,2},{4,5},{5,4},{6,7},{7,6},{8,9},{9,8},{10,11... | collective-permute-start | bytes 3080 | tf_op jit(solution)/shard_map/ppermute | solution.py:22
  172.0 27.2 %collective-permute-start.33 = (bf16[2,256]{1,0:T(2,128)(2,1)S(1)}, bf16[2,256]{1,0:T(2,128)(2,1)S(1)}, u32[]{:S(2)}, u32[]{:S(2)}) collective-permute-start(bf16[2,256]{1,0:T(2,128)(2,1)S(1)} %get-tuple-element.340), channel_id=1, source_target_pairs={{0,1},{1,0},{2,3},{3,2},{4,5},{5,4},{6,7},{7,6},{8,9},{9,8},{10,11... | collective-permute-start | bytes 3080 | tf_op jit(solution)/shard_map/ppermute | solution.py:22
  177.5 2.3 collective-permute-start.21
  179.8 18.5 %collective-permute-start.26 = (bf16[256,1024]{1,0:T(8,128)(2,1)}, bf16[256,1024]{1,0:T(8,128)(2,1)S(1)}, u32[]{:S(2)}, u32[]{:S(2)}) collective-permute-start(bf16[256,1024]{1,0:T(8,128)(2,1)} %bitcast.162), channel_id=1, source_target_pairs={{0,8},{4,12},{8,0},{12,4},{16,24},{20,28},{24,16},{28,20},{1,9},{5... | collective-permute-start | bytes 1572872 | tf_op jit(solution)/shard_map/ppermute | solution.py:22
  185.2 18.2 %collective-permute-start.25 = (bf16[256,1024]{1,0:T(8,128)(2,1)}, bf16[256,1024]{1,0:T(8,128)(2,1)}, u32[]{:S(2)}, u32[]{:S(2)}) collective-permute-start(bf16[256,1024]{1,0:T(8,128)(2,1)} %bitcast.21), channel_id=1, source_target_pairs={{0,4},{4,0},{8,12},{12,8},{16,20},{20,16},{24,28},{28,24},{1,5},{5... | collective-permute-start | bytes 1572872 | tf_op jit(solution)/shard_map/ppermute | solution.py:22
  188.6 11.2 %copy-start.27 = (bf16[2,1,128,1024]{3,2,1,0:T(8,128)(2,1)S(1)}, bf16[2,1,128,1024]{3,2,1,0:T(8,128)(2,1)}, u32[]{:S(2)}) copy-start(bf16[2,1,128,1024]{3,2,1,0:T(8,128)(2,1)} %get-tuple-element.283) | copy-start | bytes 1572868
  188.6 20.3 %collective-permute-start.24 = (bf16[256,1024]{1,0:T(8,128)(2,1)}, bf16[256,1024]{1,0:T(8,128)(2,1)S(1)}, u32[]{:S(2)}, u32[]{:S(2)}) collective-permute-start(bf16[256,1024]{1,0:T(8,128)(2,1)} %bitcast.24), channel_id=1, source_target_pairs={{0,8},{4,12},{8,0},{12,4},{16,24},{20,28},{24,16},{28,20},{1,9},{5... | collective-permute-start | bytes 1572872 | tf_op jit(solution)/shard_map/ppermute | solution.py:22
  199.2 37.1 %collective-permute-start.34 = (bf16[2,256]{1,0:T(2,128)(2,1)S(1)}, bf16[2,256]{1,0:T(2,128)(2,1)S(1)}, u32[]{:S(2)}, u32[]{:S(2)}) collective-permute-start(bf16[2,256]{1,0:T(2,128)(2,1)S(1)} %add_convert_fusion.29), channel_id=1, source_target_pairs={{0,2},{1,3},{2,0},{3,1},{4,6},{5,7},{6,4},{7,5},{8,10},{9,11},{10,... | collective-permute-start | bytes 3080 | tf_op jit(solution)/shard_map/ppermute | solution.py:22
  199.8 10.2 %copy-start.17 = (bf16[1024,1024]{1,0:T(8,128)(2,1)S(1)}, bf16[1024,1024]{1,0:T(8,128)(2,1)}, u32[]{:S(2)}) copy-start(bf16[1024,1024]{1,0:T(8,128)(2,1)} %pad_maximum_fusion.2) | copy-start | bytes 6291460
  199.8 10.2 %copy-start.63 = (bf16[1024,384]{1,0:T(8,128)(2,1)S(1)}, bf16[1024,384]{1,0:T(8,128)(2,1)}, u32[]{:S(2)}) copy-start(bf16[1024,384]{1,0:T(8,128)(2,1)} %get-tuple-element.177) | copy-start | bytes 2359300
  200.8 49.6 %collective-permute-start.41 = (bf16[128,1024]{1,0:T(8,128)(2,1)}, bf16[128,1024]{1,0:T(8,128)(2,1)}, u32[]{:S(2)}, u32[]{:S(2)}) collective-permute-start(bf16[128,1024]{1,0:T(8,128)(2,1)} %get-tuple-element.300), channel_id=1, source_target_pairs={{0,16},{4,20},{8,24},{12,28},{16,0},{20,4},{24,8},{28,12},{1,17},{... | collective-permute-start | bytes 786440 | tf_op jit(solution)/shard_map/ppermute | solution.py:22
  213.6 10.8 %copy-start.48 = (bf16[1024,128]{1,0:T(8,128)(2,1)S(1)}, bf16[1024,128]{1,0:T(8,128)(2,1)}, u32[]{:S(2)}) copy-start(bf16[1024,128]{1,0:T(8,128)(2,1)} %get-tuple-element.324) | copy-start | bytes 786436
  213.6 10.8 %copy-start.51 = (bf16[1024,128]{1,0:T(8,128)(2,1)S(1)}, bf16[1024,128]{1,0:T(8,128)(2,1)}, u32[]{:S(2)}) copy-start(bf16[1024,128]{1,0:T(8,128)(2,1)} %get-tuple-element.320) | copy-start | bytes 786436
  213.6 10.7 %copy-start.53 = (bf16[1024,128]{1,0:T(8,128)(2,1)S(1)}, bf16[1024,128]{1,0:T(8,128)(2,1)}, u32[]{:S(2)}) copy-start(bf16[1024,128]{1,0:T(8,128)(2,1)} %get-tuple-element.353) | copy-start | bytes 786436
  221.3 18.6 %collective-permute-start.39 = (bf16[128,1024]{1,0:T(8,128)(2,1)}, bf16[128,1024]{1,0:T(8,128)(2,1)}, u32[]{:S(2)}, u32[]{:S(2)}) collective-permute-start(bf16[128,1024]{1,0:T(8,128)(2,1)} %get-tuple-element.304), channel_id=1, source_target_pairs={{0,16},{4,20},{8,24},{12,28},{16,0},{20,4},{24,8},{28,12},{1,17},{... | collective-permute-start | bytes 786440 | tf_op jit(solution)/shard_map/ppermute | solution.py:22
  221.4 24.1 %collective-permute-start.40 = (bf16[128,1024]{1,0:T(8,128)(2,1)}, bf16[128,1024]{1,0:T(8,128)(2,1)}, u32[]{:S(2)}, u32[]{:S(2)}) collective-permute-start(bf16[128,1024]{1,0:T(8,128)(2,1)} %get-tuple-element.302), channel_id=1, source_target_pairs={{0,16},{4,20},{8,24},{12,28},{16,0},{20,4},{24,8},{28,12},{1,17},{... | collective-permute-start | bytes 786440 | tf_op jit(solution)/shard_map/ppermute | solution.py:22
  226.9 2.5 collective-permute-start.27
  229.4 17.9 %collective-permute-start.30 = (bf16[512,640]{1,0:T(8,128)(2,1)}, bf16[512,640]{1,0:T(8,128)(2,1)}, u32[]{:S(2)}, u32[]{:S(2)}) collective-permute-start(bf16[512,640]{1,0:T(8,128)(2,1)} %bitcast.39), channel_id=1, source_target_pairs={{0,4},{4,0},{8,12},{12,8},{16,20},{20,16},{24,28},{28,24},{1,5},{5... | collective-permute-start | bytes 1966088 | tf_op jit(solution)/shard_map/ppermute | solution.py:22
  236.4 24.0 %collective-permute-start.29 = (bf16[256,1024]{1,0:T(8,128)(2,1)}, bf16[256,1024]{1,0:T(8,128)(2,1)}, u32[]{:S(2)}, u32[]{:S(2)}) collective-permute-start(bf16[256,1024]{1,0:T(8,128)(2,1)} %add_convert_fusion.4.sent_ref), channel_id=1, source_target_pairs={{0,2},{1,3},{2,0},{3,1},{4,6},{5,7},{6,4},{7,5},{8,10},{9,11},{10,... | collective-permute-start | bytes 1572872 | tf_op jit(solution)/shard_map/ppermute | solution.py:22
  238.0 10.6 %copy-start.41 = (bf16[128,1024]{1,0:T(8,128)(2,1)S(1)}, bf16[128,1024]{1,0:T(8,128)(2,1)}, u32[]{:S(2)}) copy-start(bf16[128,1024]{1,0:T(8,128)(2,1)} %get-tuple-element.210) | copy-start | bytes 786436
  239.9 16.3 %collective-permute-start.35 = (bf16[576,384]{1,0:T(8,128)(2,1)S(1)}, bf16[576,384]{1,0:T(8,128)(2,1)S(1)}, u32[]{:S(2)}, u32[]{:S(2)}) collective-permute-start(bf16[576,384]{1,0:T(8,128)(2,1)S(1)} %bitcast.163), channel_id=1, source_target_pairs={{0,4},{4,0},{8,12},{12,8},{16,20},{20,16},{24,28},{28,24},{1,5},{5... | collective-permute-start | bytes 1327112 | tf_op jit(solution)/shard_map/ppermute | solution.py:22
  245.5 14.8 %collective-permute-start.28 = (bf16[256,1024]{1,0:T(8,128)(2,1)}, bf16[256,1024]{1,0:T(8,128)(2,1)S(1)}, u32[]{:S(2)}, u32[]{:S(2)}) collective-permute-start(bf16[256,1024]{1,0:T(8,128)(2,1)} %get-tuple-element.305), channel_id=1, source_target_pairs={{0,1},{1,0},{2,3},{3,2},{4,5},{5,4},{6,7},{7,6},{8,9},{9,8},{10,11... | collective-permute-start | bytes 1572872 | tf_op jit(solution)/shard_map/ppermute | solution.py:22
  248.5 9.8 %copy-start.40 = (bf16[128,1024]{1,0:T(8,128)(2,1)S(1)}, bf16[128,1024]{1,0:T(8,128)(2,1)}, u32[]{:S(2)}) copy-start(bf16[128,1024]{1,0:T(8,128)(2,1)} %get-tuple-element.212) | copy-start | bytes 786436
  248.5 8.9 %collective-permute-start.31 = (bf16[256,640]{1,0:T(8,128)(2,1)S(1)}, bf16[256,640]{1,0:T(8,128)(2,1)S(1)}, u32[]{:S(2)}, u32[]{:S(2)}) collective-permute-start(bf16[256,640]{1,0:T(8,128)(2,1)S(1)} %bitcast.166), channel_id=1, source_target_pairs={{0,8},{4,12},{8,0},{12,4},{16,24},{20,28},{24,16},{28,20},{1,9},{5... | collective-permute-start | bytes 983048 | tf_op jit(solution)/shard_map/ppermute | solution.py:22
  256.3 9.5 %collective-permute-start.37 = (bf16[288,384]{1,0:T(8,128)(2,1)S(1)}, bf16[288,384]{1,0:T(8,128)(2,1)S(1)}, u32[]{:S(2)}, u32[]{:S(2)}) collective-permute-start(bf16[288,384]{1,0:T(8,128)(2,1)S(1)} %bitcast.169), channel_id=1, source_target_pairs={{0,8},{4,12},{8,0},{12,4},{16,24},{20,28},{24,16},{28,20},{1,9},{5... | collective-permute-start | bytes 663560 | tf_op jit(solution)/shard_map/ppermute | solution.py:22
  258.2 9.5 %collective-permute-start.36 = (bf16[128,640]{1,0:T(8,128)(2,1)}, bf16[128,640]{1,0:T(8,128)(2,1)}, u32[]{:S(2)}, u32[]{:S(2)}) collective-permute-start(bf16[128,640]{1,0:T(8,128)(2,1)} %get-tuple-element.318), channel_id=1, source_target_pairs={{0,16},{4,20},{8,24},{12,28},{16,0},{20,4},{24,8},{28,12},{1,17},{... | collective-permute-start | bytes 491528 | tf_op jit(solution)/shard_map/ppermute | solution.py:22
  261.1 14.8 %copy-start.1 = (bf16[1024,1024]{1,0:T(8,128)(2,1)S(1)}, bf16[1024,1024]{1,0:T(8,128)(2,1)}, u32[]{:S(2)}) copy-start(bf16[1024,1024]{1,0:T(8,128)(2,1)} %param.24) | copy-start | bytes 6291460
  265.9 6.8 %collective-permute-start.38 = (bf16[144,384]{1,0:T(8,128)(2,1)S(1)}, bf16[144,384]{1,0:T(8,128)(2,1)S(1)}, u32[]{:S(2)}, u32[]{:S(2)}) collective-permute-start(bf16[144,384]{1,0:T(8,128)(2,1)S(1)} %get-tuple-element.325), channel_id=1, source_target_pairs={{0,16},{4,20},{8,24},{12,28},{16,0},{20,4},{24,8},{28,12},{1,17},{... | collective-permute-start | bytes 331784 | tf_op jit(solution)/shard_map/ppermute | solution.py:22
  (55 other events, 130.3 us)
